TPU v7x, 32 devices: a whole 2x2x4 slice. The times are simulated.
32 devices in a mesh: ia: 4 (over z), ja: 4 (over y, core), ka: 2 (over x).
Axes of the slice: x: 2, y: 2, z: 4, core: 2. Of those that a mesh axis runs over, the one named last changes fastest.
Arguments:
- tensor: float32 [8192, 8, 1024], P('ja', 'ka', 'ia'), may hold values from -6 to 6
- factor_a: float32 [1024, 128], P('ia'), may hold values from -1 to 1
- factor_c: float32 [8, 128], P('ka'), may hold values from -2 to 2
- gram_c: float32 [128, 128], replicated, may hold values from -12 to 24, as said below
Outputs:
- factor_b: float32 [8192, 128], P('ja')
- factor_c_new: float32 [8, 128], P('ka')
Inputs may be any that keep to these rules, and one draw needn't show every extreme that they name: `gram_c`: symmetric positive definite.
All inputs are finite; a program needn't handle non-finite values.
Results may differ from a plain program's by a relative error of at most 0.000071.
Values sent between devices are 32-bit elements; how exact they have to be, the bound alone decides.
A program may use at most 64 MiB of HBM per device.

v0:
```python
import functools

import jax
import jax.numpy as jnp
from jax import lax
from jax.experimental import pallas as pl
from jax.experimental.pallas import tpu as pltpu
from jax.sharding import PartitionSpec as P

HIGH = lax.Precision.HIGHEST
MESH = pl.DeviceIdType.MESH
GROUP = 16


def mm(a, b):
    return jnp.dot(a, b, precision=HIGH, preferred_element_type=jnp.float32)


def mtm(a):
    return lax.dot_general(
        a, a, (((0,), (0,)), ((), ())), precision=HIGH, preferred_element_type=jnp.float32
    )


def eliminate(a):
    n = a.shape[0]
    lane = lax.broadcasted_iota(jnp.int32, (n, n), 1)
    sub = lax.broadcasted_iota(jnp.int32, (n, n), 0)
    lane_row = lax.broadcasted_iota(jnp.int32, (1, n), 1)
    for t in range(0, GROUP, 2):
        c0 = jnp.broadcast_to(a[:, t : t + 1], (n, n))
        c1 = jnp.broadcast_to(a[:, t + 1 : t + 2], (n, n))
        p, q = c0[t : t + 1, :], c1[t : t + 1, :]
        u, s = c0[t + 1 : t + 2, :], c1[t + 1 : t + 2, :]
        inv = 1.0 / (p * s - q * u)
        here = lane_row == t
        there = lane_row == t + 1
        r0 = jnp.where(here, 1.0, jnp.where(there, 0.0, a[t : t + 1, :]))
        r1 = jnp.where(here, 0.0, jnp.where(there, 1.0, a[t + 1 : t + 2, :]))
        w0 = (s * inv) * r0 - (q * inv) * r1
        w1 = (p * inv) * r1 - (u * inv) * r0
        base = jnp.where((lane == t) | (lane == t + 1), 0.0, a)
        base = base - c0 * w0 - c1 * w1
        a = jnp.where(sub == t, w0, jnp.where(sub == t + 1, w1, base))
    a = pltpu.roll(a, n - GROUP, axis=1)
    return jnp.concatenate([a[GROUP:], a[:GROUP]], axis=0)


def scales(h):
    n = h.shape[0]
    eye = lax.broadcasted_iota(jnp.int32, (n, n), 1) == lax.broadcasted_iota(jnp.int32, (n, n), 0)
    kept = jnp.where(eye, h, 0.0)
    across = lax.rsqrt(jnp.sum(kept, axis=0, keepdims=True))
    down = lax.rsqrt(jnp.sum(kept, axis=1, keepdims=True))
    return down, across


def kernel(
    dims,
    blocks,
    t_hbm,
    a_hbm,
    c_hbm,
    gc_hbm,
    b_out,
    c_out,
    tbuf,
    part,
    mloc,
    xrecv,
    xsum,
    zrecv,
    bfull,
    ga_loc,
    ga_in,
    ga_full,
    g1,
    g1_in,
    g3,
    mj_all,
    mc_all,
    inv_ref,
    acc_ref,
    a_ref,
    c_ref,
    gc_ref,
    t_sem,
    x_send,
    x_recv,
    z_send,
    z_recv,
    p_send,
    p_recv,
    q_send,
    q_recv,
    ga_send,
    ga_recv,
    gf_send,
    gf_recv,
    g1_send,
    g1_recv,
    g3_send,
    g3_recv,
    mj_send,
    mj_recv,
    mc_send,
    mc_recv,
    o_sem,
    i_sem,
):
    ni, nj, nk = dims
    kl, rows, rank = part.shape
    jb = rows // blocks
    jx = jb // nk
    jz = jx // ni
    mi, mj, mk = lax.axis_index("ia"), lax.axis_index("ja"), lax.axis_index("ka")
    sends = []

    def peer(axis, me, n, d):
        return {axis: lax.rem(me + d, n)}

    def remote(src, dst, ss, rs, who):
        cp = pltpu.make_async_remote_copy(
            src_ref=src, dst_ref=dst, send_sem=ss, recv_sem=rs, device_id=who, device_id_type=MESH
        )
        cp.start()
        sends.append(cp)
        return cp

    icopies = []
    for n, (src, dst) in enumerate(((a_hbm, a_ref), (c_hbm, c_ref), (gc_hbm, gc_ref))):
        cp = pltpu.make_async_copy(src, dst, i_sem.at[n])
        cp.start()
        icopies.append(cp)
    tcopies = {}
    for b in range(blocks):
        for k in range(kl):
            rs = pl.ds(b * jb, jb)
            cp = pltpu.make_async_copy(t_hbm.at[rs, k, :], tbuf.at[k, rs, :], t_sem.at[b, k])
            cp.start()
            tcopies[b, k] = cp

    barrier = pltpu.get_barrier_semaphore()
    for d in range(1, ni):
        pl.semaphore_signal(barrier, inc=1, device_id=peer("ia", mi, ni, d), device_id_type=MESH)
    for d in range(1, nj):
        pl.semaphore_signal(barrier, inc=1, device_id=peer("ja", mj, nj, d), device_id_type=MESH)
    for d in range(1, nk):
        pl.semaphore_signal(barrier, inc=1, device_id=peer("ka", mk, nk, d), device_id_type=MESH)

    for cp in icopies:
        cp.wait()
    a = a_ref[...]
    a_hi = a.astype(jnp.bfloat16)
    a_lo = (a - a_hi.astype(jnp.float32)).astype(jnp.bfloat16)
    weights = jnp.concatenate([a_hi, a_lo], axis=1)
    ga_loc[...] = mtm(a)

    x_cp, z_cp, p_cp, q_cp = {}, {}, {}, {}
    step = min(256, jb)

    def first(b):
        for k in range(kl):
            tcopies[b, k].wait()

        def chunk(s, carry):
            rs = pl.ds(pl.multiple_of(b * jb + s * step, step), step)
            total = None
            for k in range(kl):
                x = tbuf[k, rs, :]
                hi = x.astype(jnp.bfloat16)
                lo = (x - hi.astype(jnp.float32)).astype(jnp.bfloat16)
                y = jnp.dot(hi, weights, preferred_element_type=jnp.float32) + jnp.dot(
                    lo, weights, preferred_element_type=jnp.float32
                )
                y = y[:, :rank] + y[:, rank:]
                part[k, rs, :] = y
                y = y * c_ref[k : k + 1, :]
                total = y if total is None else total + y
            mloc[rs, :] = total
            return carry

        lax.fori_loop(0, jb // step, chunk, 0)

    def send_first(b):
        for d in range(1, nk):
            other = lax.rem(mk + d, nk)
            rs = pl.ds(pl.multiple_of(b * jb + other * jx, 8), jx)
            x_cp[b, d] = remote(
                mloc.at[rs, :], xrecv.at[b, d - 1], x_send.at[b, d - 1], x_recv.at[b, d - 1],
                peer("ka", mk, nk, d),
            )

    hops = []
    while 2 ** len(hops) < ni:
        hops.append(2 ** len(hops))
    levels = len(hops)
    bits = [lax.rem(lax.div(mi, m), 2) for m in hops]
    starts, arrive = [0], [0]
    for n in range(levels):
        starts.append(starts[n] + bits[n] * (jx >> (n + 1)))
        arrive.append(arrive[n] + (jx >> (n + 1)))

    def across_ia(n):
        return {"ia": mi + hops[n] * (1 - 2 * bits[n])}

    def z_start(b, n):
        size = jx >> (n + 1)
        give = pl.ds(pl.multiple_of(starts[n] + (1 - bits[n]) * size, 8), size)
        z_cp[b, n] = remote(
            xsum.at[b, give, :], zrecv.at[b, pl.ds(arrive[n], size), :], z_send.at[b, n],
            z_recv.at[b, n], across_ia(n),
        )

    def z_finish(b, n):
        size = jx >> (n + 1)
        z_cp[b, n].wait_recv()
        keep = pl.ds(pl.multiple_of(starts[n + 1], 8), size)
        return keep, xsum[b, keep, :] + zrecv[b, pl.ds(arrive[n], size), :]

    def p_start(b, n):
        rs = pl.ds(pl.multiple_of(b * jb + mk * jx + starts[n + 1], 8), jx >> (n + 1))
        p_cp[b, n] = remote(
            bfull.at[rs, :], bfull.at[rs, :], p_send.at[b, n], p_recv.at[b, n], across_ia(n)
        )

    def second(b):
        total = mloc[pl.ds(pl.multiple_of(b * jb + mk * jx, 8), jx), :]
        for d in range(1, nk):
            x_cp[b, d].wait_recv()
            total = total + xrecv[b, d - 1]
        xsum[b] = total
        z_start(b, 0)

    def reduce_more(b):
        for n in range(levels - 1):
            keep, value = z_finish(b, n)
            xsum[b, keep, :] = value
            z_start(b, n + 1)

    def third(b):
        _, total = z_finish(b, levels - 1)
        rs = pl.ds(pl.multiple_of(b * jb + mk * jx + starts[levels], 8), jz)
        bfull[rs, :] = mm(total, inv_ref[...])
        p_start(b, levels - 1)

    def gather_more(b):
        for n in range(levels - 1, 0, -1):
            p_cp[b, n].wait_recv()
            p_start(b, n - 1)

    def fourth(b):
        p_cp[b, 0].wait_recv()
        rs = pl.ds(pl.multiple_of(b * jb + mk * jx, 8), jx)
        for d in range(1, nk):
            q_cp[b, d] = remote(
                bfull.at[rs, :], bfull.at[rs, :], q_send.at[b, d - 1], q_recv.at[b, d - 1],
                peer("ka", mk, nk, d),
            )

    out_cp = []

    def fifth(b):
        for d in range(1, nk):
            q_cp[b, d].wait_recv()
        rs = pl.ds(b * jb, jb)
        cp = pltpu.make_async_copy(bfull.at[rs, :], b_out.at[rs, :], o_sem.at[b])
        cp.start()
        out_cp.append(cp)
        value = bfull[rs, :]
        g1[...] = g1[...] + mtm(value)
        for k in range(kl):
            s = jnp.sum(part[k, rs, :] * value, axis=0, keepdims=True)
            acc_ref[pl.ds(k, 1), :] = acc_ref[pl.ds(k, 1), :] + s

    first(0)
    pl.semaphore_wait(barrier, ni + nj + nk - 3)
    strip = rank // nj
    part_rows = pl.ds(pl.multiple_of(mj * strip, 8), strip)
    ga_in[mi] = ga_loc[part_rows, :]
    ga_cp = [
        remote(
            ga_loc.at[part_rows, :], ga_in.at[mi], ga_send.at[d - 1], ga_recv.at[d - 1],
            peer("ia", mi, ni, d),
        )
        for d in range(1, ni)
    ]
    send_first(0)
    gf_cp = []
    for b in range(1, blocks):
        first(b)
        send_first(b)
        if b == min(2, blocks - 1):
            for cp in ga_cp:
                cp.wait_recv()
            total = ga_in[0]
            for d in range(1, ni):
                total = total + ga_in[d]
            ga_full[part_rows, :] = total
            for d in range(1, nj):
                gf_cp.append(
                    remote(
                        ga_full.at[part_rows, :], ga_full.at[part_rows, :], gf_send.at[d - 1],
                        gf_recv.at[d - 1], peer("ja", mj, nj, d),
                    )
                )

    acc_ref[...] = jnp.zeros_like(acc_ref)
    g1[...] = jnp.zeros_like(g1)
    second(0)
    for cp in gf_cp:
        cp.wait_recv()
    gram_a = ga_full[...]
    groups = rank // GROUP

    def turn(h, quarter):
        lo, hi = groups * quarter // 4, groups * (quarter + 1) // 4
        return lax.fori_loop(lo, hi, lambda _, v: eliminate(v), h)

    h = gram_a * gc_ref[...]
    down, across = scales(h)
    h = h * down * across
    h = turn(turn(h, 0), 1)
    second(1)
    reduce_more(0)
    h = turn(turn(h, 2), 3)
    inv_ref[...] = h * down * across
    stages = (second, reduce_more, third, gather_more, fourth, fifth)
    done = [2, 1, 0, 0, 0, 0]
    while done[5] < blocks:
        for n in range(6):
            if done[n] < (blocks if n == 0 else before[n - 1]):
                stages[n](done[n])
                done[n] += 1
            if n == 0:
                before = list(done)

    cut = rank // nj
    mine = pl.ds(pl.multiple_of(mj * cut, 8), cut)
    g1_in[mj] = g1[mine, :]
    g1_cp = []
    for d in range(1, nj):
        rs = pl.ds(pl.multiple_of(lax.rem(mj + d, nj) * cut, 8), cut)
        g1_cp.append(
            remote(g1.at[rs, :], g1_in.at[mj], g1_send.at[d - 1], g1_recv.at[d - 1], peer("ja", mj, nj, d))
        )
    mj_all[mj] = acc_ref[...]
    mj_cp = [
        remote(mj_all.at[mj], mj_all.at[mj], mj_send.at[d - 1], mj_recv.at[d - 1], peer("ja", mj, nj, d))
        for d in range(1, nj)
    ]
    for cp in g1_cp:
        cp.wait_recv()
    total = g1_in[0]
    for d in range(1, nj):
        total = total + g1_in[d]
    g3[mine, :] = total
    g3_cp = [
        remote(g3.at[mine, :], g3.at[mine, :], g3_send.at[d - 1], g3_recv.at[d - 1], peer("ja", mj, nj, d))
        for d in range(1, nj)
    ]
    for cp in mj_cp:
        cp.wait_recv()
    total = mj_all[0]
    for d in range(1, nj):
        total = total + mj_all[d]
    mc_all[mi] = total
    mc_cp = [
        remote(mc_all.at[mi], mc_all.at[mi], mc_send.at[d - 1], mc_recv.at[d - 1], peer("ia", mi, ni, d))
        for d in range(1, ni)
    ]
    for cp in g3_cp:
        cp.wait_recv()
    h = gram_a * g3[...]
    down, across = scales(h)
    h = h * down * across
    for quarter in range(4):
        h = turn(h, quarter)
    inverse = h * down * across
    for cp in mc_cp:
        cp.wait_recv()
    mttkrp_c = mc_all[0]
    for d in range(1, ni):
        mttkrp_c = mttkrp_c + mc_all[d]
    c_out[...] = mm(mttkrp_c, inverse)[:kl, :]
    for cp in out_cp:
        cp.wait()
    for cp in sends:
        cp.wait_send()


def body(dims, tensor, factor_a, factor_c, gram_c):
    ni, nj, nk = dims
    rows, kl, il = tensor.shape
    rank = factor_a.shape[1]
    blocks = 4
    jb = rows // blocks
    jx = jb // nk
    jz = jx // ni
    kp = -(-kl // 8) * 8
    hops = (ni - 1).bit_length()
    strip = rank // nj
    f32 = jnp.float32
    dma = pltpu.SemaphoreType.DMA
    vmem = pl.BlockSpec(memory_space=pltpu.VMEM)
    return pl.pallas_call(
        functools.partial(kernel, dims, blocks),
        out_shape=(
            jax.ShapeDtypeStruct((rows, rank), f32),
            jax.ShapeDtypeStruct((kl, rank), f32),
        ),
        in_specs=[pl.BlockSpec(memory_space=pltpu.HBM)] * 4,
        out_specs=(pl.BlockSpec(memory_space=pl.ANY), vmem),
        scratch_shapes=[
            pltpu.VMEM((kl, rows, il), f32),
            pltpu.VMEM((kl, rows, rank), f32),
            pltpu.VMEM((rows, rank), f32),
            pltpu.VMEM((blocks, nk - 1, jx, rank), f32),
            pltpu.VMEM((blocks, jx, rank), f32),
            pltpu.VMEM((blocks, jx, rank), f32),
            pltpu.VMEM((rows, rank), f32),
            pltpu.VMEM((rank, rank), f32),
            pltpu.VMEM((ni, strip, rank), f32),
            pltpu.VMEM((rank, rank), f32),
            pltpu.VMEM((rank, rank), f32),
            pltpu.VMEM((nj, rank // nj, rank), f32),
            pltpu.VMEM((rank, rank), f32),
            pltpu.VMEM((nj, kp, rank), f32),
            pltpu.VMEM((ni, kp, rank), f32),
            pltpu.VMEM((rank, rank), f32),
            pltpu.VMEM((kp, rank), f32),
            pltpu.VMEM((il, rank), f32),
            pltpu.VMEM((kl, rank), f32),
            pltpu.VMEM((rank, rank), f32),
            dma((blocks, kl)),
            dma((blocks, nk - 1)),
            dma((blocks, nk - 1)),
            dma((blocks, hops)),
            dma((blocks, hops)),
            dma((blocks, hops)),
            dma((blocks, hops)),
            dma((blocks, nk - 1)),
            dma((blocks, nk - 1)),
            dma((ni - 1,)),
            dma((ni - 1,)),
            dma((nj - 1,)),
            dma((nj - 1,)),
            dma((nj - 1,)),
            dma((nj - 1,)),
            dma((nj - 1,)),
            dma((nj - 1,)),
            dma((nj - 1,)),
            dma((nj - 1,)),
            dma((ni - 1,)),
            dma((ni - 1,)),
            dma((blocks,)),
            dma((3,)),
        ],
        compiler_params=pltpu.CompilerParams(
            collective_id=0, has_side_effects=True, vmem_limit_bytes=48 * 1024 * 1024
        ),
    )(tensor, factor_a, factor_c, gram_c)


def solution(mesh):
    dims = (mesh.shape["ia"], mesh.shape["ja"], mesh.shape["ka"])
    placed = (P("ja", "ka", "ia"), P("ia", None), P("ka", None), P())
    return jax.shard_map(
        functools.partial(body, dims),
        mesh=mesh,
        in_specs=placed,
        out_specs=(P("ja", None), P("ka", None)),
        check_vma=False,
    )
```

profile of v0, /device:TPU:0, one launch (start us, length us, event | category | flops | bytes accessed | tf_op | source)
XLA Modules:
  0.0 62.3 jit_solution(6964342248790791333)
XLA Ops:
  0.6 0.0 copy-start
  0.6 0.9 %copy-done = f32[256,128]{1,0:T(8,128)S(1)} copy-done((f32[256,128]{1,0:T(8,128)S(1)}, f32[256,128]{1,0:T(8,128)}, u32[]{:S(2)}) %copy-start) | copy-done | bytes 131096
  1.5 0.0 copy-start.1
  1.5 0.8 %copy-done.1 = f32[128,128]{1,0:T(8,128)S(1)} copy-done((f32[128,128]{1,0:T(8,128)S(1)}, f32[128,128]{1,0:T(8,128)}, u32[]{:S(2)}) %copy-start.1) | copy-done | bytes 65560
  2.4 0.0 copy-start.2
  2.4 0.7 %copy-done.2 = f32[4,128]{1,0:T(4,128)S(1)} copy-done((f32[4,128]{1,0:T(4,128)S(1)}, f32[4,128]{1,0:T(4,128)}, u32[]{:S(2)}) %copy-start.2) | copy-done | bytes 2072
  3.1 57.7 %shard_map.59 = (f32[2048,128]{1,0:T(8,128)S(1)}, f32[4,128]{1,0:T(4,128)S(1)}) custom-call(f32[2048,4,256]{2,1,0:T(4,128)} %t_hbm.1, f32[256,128]{1,0:T(8,128)S(1)} %copy-done, f32[4,128]{1,0:T(4,128)S(1)} %copy-done.2, f32[128,128]{1,0:T(8,128)S(1)} %copy-done.1), custom_call_target="tpu_custom_call" | custom-call | tf_op jit(solution)/shard_map/pallas_call | solution.py:406
  60.8 1.0 %copy.8 = f32[2048,128]{1,0:T(8,128)} copy(f32[2048,128]{1,0:T(8,128)S(1)} %get-tuple-element.4) | data formatting | bytes 2097152
  61.7 0.6 copy.9
Async XLA Ops:
  0.6 0.9 %copy-start = (f32[256,128]{1,0:T(8,128)S(1)}, f32[256,128]{1,0:T(8,128)}, u32[]{:S(2)}) copy-start(f32[256,128]{1,0:T(8,128)} %a_hbm.1) | copy-start | bytes 393220
  1.5 0.8 %copy-start.1 = (f32[128,128]{1,0:T(8,128)S(1)}, f32[128,128]{1,0:T(8,128)}, u32[]{:S(2)}) copy-start(f32[128,128]{1,0:T(8,128)} %gc_hbm.1) | copy-start | bytes 196612
  2.4 0.7 %copy-start.2 = (f32[4,128]{1,0:T(4,128)S(1)}, f32[4,128]{1,0:T(4,128)}, u32[]{:S(2)}) copy-start(f32[4,128]{1,0:T(4,128)} %c_hbm.1) | copy-start | bytes 6148
where the time goes:
time: 62.5 us; the launch traced here: 62.3 us
  Pallas kernels  57.7 us (92%)
  local copies, waits for them, and re-layouts  3.97 us (6%)
  between operations  0.65 us (1%)
    pallas_call x1, Pallas kernels, body(): pl.pallas_call(functools.partial(kernel, dims, blocks), out_shape=(jax.Sh...  57.7 us
    unnamed x8, local copies, waits for them, and re-layouts  3.97 us

commit v1 on v0

--- a/solution.py
+++ b/solution.py
@@ -9,11 +9,37 @@
 
 HIGH = lax.Precision.HIGHEST
 MESH = pl.DeviceIdType.MESH
-GROUP = 16
+PANEL = 64
+WARM, FIRST, BEGIN, X_TIME, HOP = 2.0, 3.7, 3.0, 11.4, 2.5
+LAG = (2.2, 3.0, 2.9, 2.3, 0.0)
+REDUCE_AT, GRAM_AT, UNIT = 6.3, 9.5, 0.35
+PIECE = 8
 
 
 def mm(a, b):
     return jnp.dot(a, b, precision=HIGH, preferred_element_type=jnp.float32)
+
+
+def split3(x):
+    a = x.astype(jnp.bfloat16)
+    x = x - a.astype(jnp.float32)
+    b = x.astype(jnp.bfloat16)
+    c = (x - b.astype(jnp.float32)).astype(jnp.bfloat16)
+    return a, b, c
+
+
+def pack_right(w):
+    b1, b2, b3 = split3(w)
+    top = jnp.concatenate([b1, b2], axis=1)
+    return jnp.concatenate([top, top], axis=0), jnp.concatenate([b1, b3], axis=0)
+
+
+def mm_packed(x, first, second):
+    n = second.shape[1]
+    a1, a2, a3 = split3(x)
+    y = jnp.dot(jnp.concatenate([a1, a2], axis=1), first, preferred_element_type=jnp.float32)
+    z = jnp.dot(jnp.concatenate([a3, a1], axis=1), second, preferred_element_type=jnp.float32)
+    return y[:, :n] + (y[:, n:] + z)
 
 
 def mtm(a):
@@ -22,28 +48,94 @@
     )
 
 
-def eliminate(a):
+def take_pivots(rows, q, at):
+    n = rows[0].shape[1]
+    lane = lax.broadcasted_iota(jnp.int32, (PIECE, n), 1)
+    sub = lax.broadcasted_iota(jnp.int32, (PIECE, n), 0)
+    lane_row = lax.broadcasted_iota(jnp.int32, (1, n), 1)
+    order = [q] + [v for v in range(len(rows)) if v != q]
+    cols = {
+        v: [jnp.broadcast_to(rows[v][:, at + j : at + j + 1], (PIECE, n)) for j in range(PIECE)]
+        for v in order
+    }
+    x, ahead = rows[q], list(cols[q])
+    for t in range(0, PIECE, 2):
+        c0, c1 = ahead[t], ahead[t + 1]
+        p, r = c0[t : t + 1], c1[t : t + 1]
+        u, s = c0[t + 1 : t + 2], c1[t + 1 : t + 2]
+        inv = 1.0 / (p * s - r * u)
+
+        def step(y0, y1, kept):
+            w0 = (s * y0 - r * y1) * inv
+            w1 = (p * y1 - u * y0) * inv
+            rest = kept - c0 * w0 - c1 * w1
+            return jnp.where(sub == t, w0, jnp.where(sub == t + 1, w1, rest))
+
+        for j in range(t + 2, PIECE):
+            y = ahead[j]
+            ahead[j] = step(y[t : t + 1], y[t + 1 : t + 2], y)
+        here, there = lane_row == at + t, lane_row == at + t + 1
+        y0 = jnp.where(here, 1.0, jnp.where(there, 0.0, x[t : t + 1]))
+        y1 = jnp.where(here, 0.0, jnp.where(there, 1.0, x[t + 1 : t + 2]))
+        x = step(y0, y1, jnp.where((lane == at + t) | (lane == at + t + 1), 0.0, x))
+    own = (lane >= at) & (lane < at + PIECE)
+    out = list(rows)
+    out[q] = x
+    for v in order[1:]:
+        terms = [cols[v][j] * x[j : j + 1] for j in range(PIECE)]
+        while len(terms) > 1:
+            terms = [terms[i] + terms[i + 1] for i in range(0, len(terms), 2)]
+        out[v] = jnp.where(own, 0.0, rows[v]) - terms[0]
+    return out
+
+
+def inverse_steps(a):
     n = a.shape[0]
     lane = lax.broadcasted_iota(jnp.int32, (n, n), 1)
     sub = lax.broadcasted_iota(jnp.int32, (n, n), 0)
-    lane_row = lax.broadcasted_iota(jnp.int32, (1, n), 1)
-    for t in range(0, GROUP, 2):
-        c0 = jnp.broadcast_to(a[:, t : t + 1], (n, n))
-        c1 = jnp.broadcast_to(a[:, t + 1 : t + 2], (n, n))
-        p, q = c0[t : t + 1, :], c1[t : t + 1, :]
-        u, s = c0[t + 1 : t + 2, :], c1[t + 1 : t + 2, :]
-        inv = 1.0 / (p * s - q * u)
-        here = lane_row == t
-        there = lane_row == t + 1
-        r0 = jnp.where(here, 1.0, jnp.where(there, 0.0, a[t : t + 1, :]))
-        r1 = jnp.where(here, 0.0, jnp.where(there, 1.0, a[t + 1 : t + 2, :]))
-        w0 = (s * inv) * r0 - (q * inv) * r1
-        w1 = (p * inv) * r1 - (u * inv) * r0
-        base = jnp.where((lane == t) | (lane == t + 1), 0.0, a)
-        base = base - c0 * w0 - c1 * w1
-        a = jnp.where(sub == t, w0, jnp.where(sub == t + 1, w1, base))
-    a = pltpu.roll(a, n - GROUP, axis=1)
-    return jnp.concatenate([a[GROUP:], a[:GROUP]], axis=0)
+    for base in range(0, n, PANEL):
+        rows = [a[base + m : base + m + PIECE] for m in range(0, PANEL, PIECE)]
+        for q in range(len(rows)):
+            rows = take_pivots(rows, q, base + PIECE * q)
+            if q + 1 < len(rows):
+                yield None
+        pieces = [jnp.zeros((base, n), jnp.float32)] if base else []
+        pieces += rows
+        if base + PANEL < n:
+            pieces.append(jnp.zeros((n - base - PANEL, n), jnp.float32))
+        done = jnp.concatenate(pieces, axis=0)
+        inside = (lane >= base) & (lane < base + PANEL)
+        factor = jnp.where(inside, a, 0.0)
+        rest = jnp.where(inside, 0.0, a) - mm_packed(factor, *pack_right(done))
+        a = jnp.where((sub >= base) & (sub < base + PANEL), done, rest)
+        yield a
+
+
+def inverse(a):
+    for a in inverse_steps(a):
+        pass
+    return a
+
+
+def plan(blocks, units):
+    pace = X_TIME / blocks
+    events = []
+    ready = [0.0] * blocks
+    for b in range(blocks):
+        events.append((WARM + FIRST / blocks * (b + 1), b, "first", b))
+        t = BEGIN + pace * (b + 1) + HOP
+        for n, name in enumerate(("second", "reduce_more", "third", "gather_more", "fourth")):
+            events.append((t, b, name, b))
+            ready[b] = t
+            t += LAG[n]
+    link = BEGIN + X_TIME
+    for b in range(blocks):
+        link = max(link, ready[b]) + pace
+        events.append((link + HOP, b, "fifth", b))
+    events.append((REDUCE_AT, blocks, "gram_reduce", None))
+    for n in range(units):
+        events.append((GRAM_AT + n * UNIT, blocks, "side", None))
+    return [(name, b) for _, _, name, b in sorted(events, key=lambda e: e[:2])]
 
 
 def scales(h):
@@ -70,16 +162,18 @@
     xrecv,
     xsum,
     zrecv,
+    mfull,
     bfull,
     ga_loc,
     ga_in,
     ga_full,
     g1,
-    g1_in,
+    g_in,
+    g_out,
     g3,
-    mj_all,
     mc_all,
-    inv_ref,
+    inv_a,
+    inv_b,
     acc_ref,
     a_ref,
     c_ref,
@@ -97,12 +191,8 @@
     ga_recv,
     gf_send,
     gf_recv,
-    g1_send,
-    g1_recv,
-    g3_send,
-    g3_recv,
-    mj_send,
-    mj_recv,
+    g_send,
+    g_recv,
     mc_send,
     mc_recv,
     o_sem,
@@ -221,7 +311,7 @@
     def p_start(b, n):
         rs = pl.ds(pl.multiple_of(b * jb + mk * jx + starts[n + 1], 8), jx >> (n + 1))
         p_cp[b, n] = remote(
-            bfull.at[rs, :], bfull.at[rs, :], p_send.at[b, n], p_recv.at[b, n], across_ia(n)
+            mfull.at[rs, :], mfull.at[rs, :], p_send.at[b, n], p_recv.at[b, n], across_ia(n)
         )
 
     def second(b):
@@ -241,7 +331,7 @@
     def third(b):
         _, total = z_finish(b, levels - 1)
         rs = pl.ds(pl.multiple_of(b * jb + mk * jx + starts[levels], 8), jz)
-        bfull[rs, :] = mm(total, inv_ref[...])
+        mfull[rs, :] = total
         p_start(b, levels - 1)
 
     def gather_more(b):
@@ -254,7 +344,7 @@
         rs = pl.ds(pl.multiple_of(b * jb + mk * jx, 8), jx)
         for d in range(1, nk):
             q_cp[b, d] = remote(
-                bfull.at[rs, :], bfull.at[rs, :], q_send.at[b, d - 1], q_recv.at[b, d - 1],
+                mfull.at[rs, :], mfull.at[rs, :], q_send.at[b, d - 1], q_recv.at[b, d - 1],
                 peer("ka", mk, nk, d),
             )
 
@@ -264,16 +354,24 @@
         for d in range(1, nk):
             q_cp[b, d].wait_recv()
         rs = pl.ds(b * jb, jb)
+        value = mm_packed(mfull[rs, :], inv_a[...], inv_b[...])
+        bfull[rs, :] = value
+        gram = mtm(value)
+        g1[...] = gram if b == 0 else g1[...] + gram
+        return value
+
+    def sixth(b, value):
+        rs = pl.ds(b * jb, jb)
+        for k in range(kl):
+            s = jnp.sum(part[k, rs, :] * value, axis=0, keepdims=True)
+            acc_ref[pl.ds(k, 1), :] = acc_ref[pl.ds(k, 1), :] + s
         cp = pltpu.make_async_copy(bfull.at[rs, :], b_out.at[rs, :], o_sem.at[b])
         cp.start()
         out_cp.append(cp)
-        value = bfull[rs, :]
-        g1[...] = g1[...] + mtm(value)
-        for k in range(kl):
-            s = jnp.sum(part[k, rs, :] * value, axis=0, keepdims=True)
-            acc_ref[pl.ds(k, 1), :] = acc_ref[pl.ds(k, 1), :] + s
-
-    first(0)
+
+    ahead = min(2, blocks)
+    for b in range(ahead):
+        first(b)
     pl.semaphore_wait(barrier, ni + nj + nk - 3)
     strip = rank // nj
     part_rows = pl.ds(pl.multiple_of(mj * strip, 8), strip)
@@ -285,115 +383,161 @@
         )
         for d in range(1, ni)
     ]
-    send_first(0)
+    for b in range(ahead):
+        send_first(b)
     gf_cp = []
-    for b in range(1, blocks):
-        first(b)
-        send_first(b)
-        if b == min(2, blocks - 1):
-            for cp in ga_cp:
-                cp.wait_recv()
-            total = ga_in[0]
-            for d in range(1, ni):
-                total = total + ga_in[d]
-            ga_full[part_rows, :] = total
-            for d in range(1, nj):
-                gf_cp.append(
-                    remote(
-                        ga_full.at[part_rows, :], ga_full.at[part_rows, :], gf_send.at[d - 1],
-                        gf_recv.at[d - 1], peer("ja", mj, nj, d),
-                    )
+    state = {}
+
+    def gram_reduce():
+        for cp in ga_cp:
+            cp.wait_recv()
+        total = ga_in[0]
+        for d in range(1, ni):
+            total = total + ga_in[d]
+        ga_full[part_rows, :] = total
+        for d in range(1, nj):
+            gf_cp.append(
+                remote(
+                    ga_full.at[part_rows, :], ga_full.at[part_rows, :], gf_send.at[d - 1],
+                    gf_recv.at[d - 1], peer("ja", mj, nj, d),
                 )
+            )
+
+    def side_steps():
+        for cp in gf_cp:
+            cp.wait_recv()
+        h = ga_full[...] * gc_ref[...]
+        down, across = scales(h)
+        for h in inverse_steps(h * down * across):
+            yield
+        inv_a[...], inv_b[...] = pack_right(h * down * across)
+        yield
 
     acc_ref[...] = jnp.zeros_like(acc_ref)
-    g1[...] = jnp.zeros_like(g1)
-    second(0)
-    for cp in gf_cp:
+    units = rank // PIECE + 1
+    side = side_steps()
+    left = units
+
+    def advance(count):
+        for _ in range(count):
+            next(side)
+
+    for name, b in plan(blocks, units):
+        if name == "first":
+            if b >= ahead:
+                first(b)
+                send_first(b)
+        elif name == "gram_reduce":
+            gram_reduce()
+        elif name == "side":
+            if left:
+                advance(1)
+                left -= 1
+        elif name == "fifth":
+            advance(left)
+            left = 0
+            value = fifth(b)
+            if b + 1 < blocks:
+                sixth(b, value)
+        else:
+            {
+                "second": second,
+                "reduce_more": reduce_more,
+                "third": third,
+                "gather_more": gather_more,
+                "fourth": fourth,
+            }[name](b)
+
+    half = rank // 2
+    low = lax.rem(mj, 2)
+    mine = pl.ds(pl.multiple_of(low * half, 8), half)
+    other = pl.ds(pl.multiple_of((1 - low) * half, 8), half)
+    partner = {"ja": mj + 1 - 2 * low}
+    cp = remote(g1.at[other, :], g_in.at[0], g_send.at[0], g_recv.at[0], partner)
+    sixth(blocks - 1, value)
+    mc_all[mi * nj + mj] = acc_ref[...]
+    mc_cp = []
+    for d in range(ni):
+        for e in range(nj):
+            if d + e:
+                where = {**peer("ia", mi, ni, d), **peer("ja", mj, nj, e)}
+                n = d * nj + e - 1
+                slot = mc_all.at[mi * nj + mj]
+                mc_cp.append(remote(slot, slot, mc_send.at[n], mc_recv.at[n], where))
+    cp.wait_recv()
+    total = g1[mine, :] + g_in[0]
+    level = 1
+    while 2**level < nj:
+        hop = 2**level
+        bit = lax.rem(lax.div(mj, hop), 2)
+        g_out[level - 1] = total
+        cp = remote(
+            g_out.at[level - 1], g_in.at[level], g_send.at[level], g_recv.at[level],
+            {"ja": mj + hop * (1 - 2 * bit)},
+        )
         cp.wait_recv()
-    gram_a = ga_full[...]
-    groups = rank // GROUP
-
-    def turn(h, quarter):
-        lo, hi = groups * quarter // 4, groups * (quarter + 1) // 4
-        return lax.fori_loop(lo, hi, lambda _, v: eliminate(v), h)
-
-    h = gram_a * gc_ref[...]
+        total = total + g_in[level]
+        level += 1
+    g3[mine, :] = total
+    cp = remote(g3.at[mine, :], g3.at[mine, :], g_send.at[level], g_recv.at[level], partner)
+    cp.wait_recv()
+    h = ga_full[...] * g3[...]
     down, across = scales(h)
     h = h * down * across
-    h = turn(turn(h, 0), 1)
-    second(1)
-    reduce_more(0)
-    h = turn(turn(h, 2), 3)
-    inv_ref[...] = h * down * across
-    stages = (second, reduce_more, third, gather_more, fourth, fifth)
-    done = [2, 1, 0, 0, 0, 0]
-    while done[5] < blocks:
-        for n in range(6):
-            if done[n] < (blocks if n == 0 else before[n - 1]):
-                stages[n](done[n])
-                done[n] += 1
-            if n == 0:
-                before = list(done)
-
-    cut = rank // nj
-    mine = pl.ds(pl.multiple_of(mj * cut, 8), cut)
-    g1_in[mj] = g1[mine, :]
-    g1_cp = []
-    for d in range(1, nj):
-        rs = pl.ds(pl.multiple_of(lax.rem(mj + d, nj) * cut, 8), cut)
-        g1_cp.append(
-            remote(g1.at[rs, :], g1_in.at[mj], g1_send.at[d - 1], g1_recv.at[d - 1], peer("ja", mj, nj, d))
-        )
-    mj_all[mj] = acc_ref[...]
-    mj_cp = [
-        remote(mj_all.at[mj], mj_all.at[mj], mj_send.at[d - 1], mj_recv.at[d - 1], peer("ja", mj, nj, d))
-        for d in range(1, nj)
-    ]
-    for cp in g1_cp:
-        cp.wait_recv()
-    total = g1_in[0]
-    for d in range(1, nj):
-        total = total + g1_in[d]
-    g3[mine, :] = total
-    g3_cp = [
-        remote(g3.at[mine, :], g3.at[mine, :], g3_send.at[d - 1], g3_recv.at[d - 1], peer("ja", mj, nj, d))
-        for d in range(1, nj)
-    ]
-    for cp in mj_cp:
-        cp.wait_recv()
-    total = mj_all[0]
-    for d in range(1, nj):
-        total = total + mj_all[d]
-    mc_all[mi] = total
-    mc_cp = [
-        remote(mc_all.at[mi], mc_all.at[mi], mc_send.at[d - 1], mc_recv.at[d - 1], peer("ia", mi, ni, d))
-        for d in range(1, ni)
-    ]
-    for cp in g3_cp:
-        cp.wait_recv()
-    h = gram_a * g3[...]
-    down, across = scales(h)
-    h = h * down * across
-    for quarter in range(4):
-        h = turn(h, quarter)
-    inverse = h * down * across
+    first_w, second_w = pack_right(inverse(h) * down * across)
     for cp in mc_cp:
         cp.wait_recv()
     mttkrp_c = mc_all[0]
-    for d in range(1, ni):
-        mttkrp_c = mttkrp_c + mc_all[d]
-    c_out[...] = mm(mttkrp_c, inverse)[:kl, :]
+    for n in range(1, ni * nj):
+        mttkrp_c = mttkrp_c + mc_all[n]
+    c_out[...] = mm_packed(mttkrp_c, first_w, second_w)[:kl, :]
     for cp in out_cp:
         cp.wait()
     for cp in sends:
         cp.wait_send()
 
 
+def pass_on(pieces, b_in, c_in, b_out, c_out, b_ref, c_ref, load, store):
+    size = b_ref.shape[0] // pieces
+    cuts = [pl.ds(n * size, size) for n in range(pieces)]
+    moves = [(b_in.at[cut, :], b_ref.at[cut, :], b_out.at[cut, :]) for cut in cuts]
+    moves.insert(0, (c_in, c_ref, c_out))
+    loads = [pltpu.make_async_copy(m[0], m[1], load.at[n]) for n, m in enumerate(moves)]
+    stores = [pltpu.make_async_copy(m[1], m[2], store.at[n]) for n, m in enumerate(moves)]
+    for cp in loads:
+        cp.start()
+    for one, two in zip(loads, stores):
+        one.wait()
+        two.start()
+    for cp in stores:
+        cp.wait()
+
+
+def deliver(b, c):
+    pieces = 4
+    hbm = pl.BlockSpec(memory_space=pltpu.HBM)
+    dma = pltpu.SemaphoreType.DMA
+    return pl.pallas_call(
+        functools.partial(pass_on, pieces),
+        out_shape=(jax.ShapeDtypeStruct(b.shape, b.dtype), jax.ShapeDtypeStruct(c.shape, c.dtype)),
+        in_specs=[hbm, hbm],
+        out_specs=(hbm, hbm),
+        scratch_shapes=[
+            pltpu.VMEM(b.shape, b.dtype),
+            pltpu.VMEM(c.shape, c.dtype),
+            dma((pieces + 1,)),
+            dma((pieces + 1,)),
+        ],
+        compiler_params=pltpu.CompilerParams(vmem_limit_bytes=60 * 1024 * 1024),
+    )(b, c)
+
+
 def body(dims, tensor, factor_a, factor_c, gram_c):
     ni, nj, nk = dims
     rows, kl, il = tensor.shape
     rank = factor_a.shape[1]
-    blocks = 4
+    blocks = min(8, rows // (8 * nk * ni))
+    levels = (nj - 1).bit_length()
     jb = rows // blocks
     jx = jb // nk
     jz = jx // ni
@@ -403,7 +547,7 @@
     f32 = jnp.float32
     dma = pltpu.SemaphoreType.DMA
     vmem = pl.BlockSpec(memory_space=pltpu.VMEM)
-    return pl.pallas_call(
+    b, c = pl.pallas_call(
         functools.partial(kernel, dims, blocks),
         out_shape=(
             jax.ShapeDtypeStruct((rows, rank), f32),
@@ -419,15 +563,17 @@
             pltpu.VMEM((blocks, jx, rank), f32),
             pltpu.VMEM((blocks, jx, rank), f32),
             pltpu.VMEM((rows, rank), f32),
+            pltpu.VMEM((rows, rank), f32),
             pltpu.VMEM((rank, rank), f32),
             pltpu.VMEM((ni, strip, rank), f32),
             pltpu.VMEM((rank, rank), f32),
             pltpu.VMEM((rank, rank), f32),
-            pltpu.VMEM((nj, rank // nj, rank), f32),
+            pltpu.VMEM((levels, rank // 2, rank), f32),
+            pltpu.VMEM((levels, rank // 2, rank), f32),
             pltpu.VMEM((rank, rank), f32),
-            pltpu.VMEM((nj, kp, rank), f32),
-            pltpu.VMEM((ni, kp, rank), f32),
-            pltpu.VMEM((rank, rank), f32),
+            pltpu.VMEM((ni * nj, kp, rank), f32),
+            pltpu.VMEM((2 * rank, 2 * rank), jnp.bfloat16),
+            pltpu.VMEM((2 * rank, rank), jnp.bfloat16),
             pltpu.VMEM((kp, rank), f32),
             pltpu.VMEM((il, rank), f32),
             pltpu.VMEM((kl, rank), f32),
@@ -445,21 +591,18 @@
             dma((ni - 1,)),
             dma((nj - 1,)),
             dma((nj - 1,)),
-            dma((nj - 1,)),
-            dma((nj - 1,)),
-            dma((nj - 1,)),
-            dma((nj - 1,)),
-            dma((nj - 1,)),
-            dma((nj - 1,)),
-            dma((ni - 1,)),
-            dma((ni - 1,)),
+            dma((levels + 1,)),
+            dma((levels + 1,)),
+            dma((ni * nj - 1,)),
+            dma((ni * nj - 1,)),
             dma((blocks,)),
             dma((3,)),
         ],
         compiler_params=pltpu.CompilerParams(
-            collective_id=0, has_side_effects=True, vmem_limit_bytes=48 * 1024 * 1024
+            collective_id=0, has_side_effects=True, vmem_limit_bytes=60 * 1024 * 1024
         ),
     )(tensor, factor_a, factor_c, gram_c)
+    return deliver(b, c)
 
 
 def solution(mesh):

time: 62.5 us -> 54.2 us (0.87)
  Pallas kernels: 57.7 us -> 53.4 us
  local copies, waits for them, and re-layouts: 3.97 us -> 0 us
    pallas_call x1, Pallas kernels: 57.7 us -> 51.4 us  [body(): pl.pallas_call(functools.partial(kernel, dims, blocks), out_shape=(jax.Sh...]
    unnamed x8 -> x0, local copies, waits for them, and re-layouts: 3.97 us -> none
    pallas_call x0 -> x1, Pallas kernels: none -> 2 us  [deliver(): pl.pallas_call(functools.partial(pass_on, pieces), out_shape=(jax.ShapeDt...]
where the time goes in v1:
time: 54.2 us; the launch traced here: 54 us
  Pallas kernels  53.4 us (99%)
  between operations  0.64 us (1%)
    pallas_call x1, Pallas kernels, body(): pl.pallas_call(functools.partial(kernel, dims, blocks), out_shape=(jax.Sh...  51.4 us
    pallas_call x1, Pallas kernels, deliver(): pl.pallas_call(functools.partial(pass_on, pieces), out_shape=(jax.ShapeDt...  2 us

profile of v1, /device:TPU:0, one launch (start us, length us, event | category | flops | bytes accessed | tf_op | source)
XLA Modules:
  0.0 54.0 jit_solution(1303303680873562767)
XLA Ops:
  0.6 51.4 %shard_map.59 = (f32[2048,128]{1,0:T(8,128)}, f32[4,128]{1,0:T(4,128)}) custom-call(f32[2048,4,256]{2,1,0:T(4,128)} %t_hbm.1, f32[256,128]{1,0:T(8,128)} %a_hbm.1, f32[4,128]{1,0:T(4,128)} %c_hbm.1, f32[128,128]{1,0:T(8,128)} %gc_hbm.1), custom_call_target="tpu_custom_call" | custom-call | tf_op jit(solution)/shard_map/pallas_call | solution.py:550
  52.0 2.0 %shard_map.60 = (f32[2048,128]{1,0:T(8,128)}, f32[4,128]{1,0:T(4,128)}) custom-call(f32[2048,128]{1,0:T(8,128)} %get-tuple-element.4.b_in, f32[4,128]{1,0:T(4,128)} %get-tuple-element.5.c_in), custom_call_target="tpu_custom_call" | custom-call | tf_op jit(solution)/shard_map/pallas_call | solution.py:520

commit v2 on v1

--- a/solution.py
+++ b/solution.py
@@ -11,9 +11,11 @@
 MESH = pl.DeviceIdType.MESH
 PANEL = 64
 WARM, FIRST, BEGIN, X_TIME, HOP = 2.0, 3.7, 3.0, 11.4, 2.5
-LAG = (2.2, 3.0, 2.9, 2.3, 0.0)
+LAG = (3.2, 3.2, 3.2, 3.2, 0.0)
 REDUCE_AT, GRAM_AT, UNIT = 6.3, 9.5, 0.35
 PIECE = 8
+NB = 16
+KL = 56 * 1024 * 1024
 
 
 def mm(a, b):
@@ -117,21 +119,24 @@
     return a
 
 
-def plan(blocks, units):
+def plan(blocks, groups, units):
     pace = X_TIME / blocks
     events = []
     ready = [0.0] * blocks
+    per = blocks // groups
+    for g in range(groups):
+        events.append((WARM + FIRST / groups * (g + 1), g * per, "first", g))
     for b in range(blocks):
-        events.append((WARM + FIRST / blocks * (b + 1), b, "first", b))
         t = BEGIN + pace * (b + 1) + HOP
-        for n, name in enumerate(("second", "reduce_more", "third", "gather_more", "fourth")):
+        for n, name in enumerate(("second", "fold", "third", "center_done", "outer_done")):
             events.append((t, b, name, b))
             ready[b] = t
             t += LAG[n]
     link = BEGIN + X_TIME
     for b in range(blocks):
         link = max(link, ready[b]) + pace
-        events.append((link + HOP, b, "fifth", b))
+        if b % per == per - 1:
+            events.append((link + HOP, b, "fifth", b // per))
     events.append((REDUCE_AT, blocks, "gram_reduce", None))
     for n in range(units):
         events.append((GRAM_AT + n * UNIT, blocks, "side", None))
@@ -150,6 +155,7 @@
 def kernel(
     dims,
     blocks,
+    groups,
     t_hbm,
     a_hbm,
     c_hbm,
@@ -162,8 +168,8 @@
     xrecv,
     xsum,
     zrecv,
+    zhalf,
     mfull,
-    bfull,
     ga_loc,
     ga_in,
     ga_full,
@@ -195,24 +201,27 @@
     g_recv,
     mc_send,
     mc_recv,
-    o_sem,
     i_sem,
 ):
     ni, nj, nk = dims
     kl, rows, rank = part.shape
     jb = rows // blocks
     jx = jb // nk
-    jz = jx // ni
+    jg = rows // groups
+    per = blocks // groups
     mi, mj, mk = lax.axis_index("ia"), lax.axis_index("ja"), lax.axis_index("ka")
     sends = []
 
     def peer(axis, me, n, d):
         return {axis: lax.rem(me + d, n)}
 
-    def remote(src, dst, ss, rs, who):
-        cp = pltpu.make_async_remote_copy(
+    def planned(src, dst, ss, rs, who):
+        return pltpu.make_async_remote_copy(
             src_ref=src, dst_ref=dst, send_sem=ss, recv_sem=rs, device_id=who, device_id_type=MESH
         )
+
+    def remote(src, dst, ss, rs, who):
+        cp = planned(src, dst, ss, rs, who)
         cp.start()
         sends.append(cp)
         return cp
@@ -223,9 +232,9 @@
         cp.start()
         icopies.append(cp)
     tcopies = {}
-    for b in range(blocks):
+    for b in range(groups):
         for k in range(kl):
-            rs = pl.ds(b * jb, jb)
+            rs = pl.ds(b * jg, jg)
             cp = pltpu.make_async_copy(t_hbm.at[rs, k, :], tbuf.at[k, rs, :], t_sem.at[b, k])
             cp.start()
             tcopies[b, k] = cp
@@ -247,14 +256,14 @@
     ga_loc[...] = mtm(a)
 
     x_cp, z_cp, p_cp, q_cp = {}, {}, {}, {}
-    step = min(256, jb)
+    step = min(256, jg)
 
     def first(b):
         for k in range(kl):
             tcopies[b, k].wait()
 
         def chunk(s, carry):
-            rs = pl.ds(pl.multiple_of(b * jb + s * step, step), step)
+            rs = pl.ds(pl.multiple_of(b * jg + s * step, step), step)
             total = None
             for k in range(kl):
                 x = tbuf[k, rs, :]
@@ -270,106 +279,140 @@
             mloc[rs, :] = total
             return carry
 
-        lax.fori_loop(0, jb // step, chunk, 0)
-
-    def send_first(b):
+        lax.fori_loop(0, jg // step, chunk, 0)
+
+    def send_first(g):
+        for b in range(g * per, g * per + per):
+            for d in range(1, nk):
+                other = lax.rem(mk + d, nk)
+                rs = pl.ds(pl.multiple_of(b * jb + other * jx, 8), jx)
+                x_cp[b, d] = remote(
+                    mloc.at[rs, :], xrecv.at[b, d - 1], x_send.at[b, d - 1], x_recv.at[b, d - 1],
+                    peer("ka", mk, nk, d),
+                )
+
+    def own_rows(b, at, size):
+        return pl.ds(pl.multiple_of(b * jb + mk * jx + at, 8), size)
+
+    middle = ni // 2
+    low_side = mi < middle
+    is_center = (mi == middle - 1) | (mi == middle)
+    has_outer = (mi > 0) & (mi < ni - 1)
+    inward = {"ia": jnp.clip(jnp.where(low_side, mi + 1, mi - 1), 0, ni - 1)}
+    outward = {"ia": jnp.clip(jnp.where(low_side, mi - 1, mi + 1), 0, ni - 1)}
+    across = {"ia": ni - 1 - mi}
+    jh = jx // 2
+    keep = jnp.where(low_side, 0, jh)
+    give = jh - keep
+    fold_cp, part_cp, half_cp, unfold_cp = {}, {}, {}, {}
+    for b in range(blocks):
+        fold_cp[b] = planned(
+            xsum.at[b], zrecv.at[b], z_send.at[b, 0], z_recv.at[b, 0], inward
+        )
+        part_cp[b] = planned(
+            xsum.at[b, pl.ds(pl.multiple_of(give, 8), jh), :], zhalf.at[b],
+            z_send.at[b, 1], z_recv.at[b, 1], across,
+        )
+        rs = own_rows(b, keep, jh)
+        half_cp[b] = planned(
+            mfull.at[rs, :], mfull.at[rs, :], p_send.at[b, 0], p_recv.at[b, 0], across
+        )
+        rs = own_rows(b, 0, jx)
+        unfold_cp[b] = planned(
+            mfull.at[rs, :], mfull.at[rs, :], p_send.at[b, 1], p_recv.at[b, 1], outward
+        )
         for d in range(1, nk):
-            other = lax.rem(mk + d, nk)
-            rs = pl.ds(pl.multiple_of(b * jb + other * jx, 8), jx)
-            x_cp[b, d] = remote(
-                mloc.at[rs, :], xrecv.at[b, d - 1], x_send.at[b, d - 1], x_recv.at[b, d - 1],
+            q_cp[b, d] = planned(
+                mfull.at[rs, :], mfull.at[rs, :], q_send.at[b, d - 1], q_recv.at[b, d - 1],
                 peer("ka", mk, nk, d),
             )
-
-    hops = []
-    while 2 ** len(hops) < ni:
-        hops.append(2 ** len(hops))
-    levels = len(hops)
-    bits = [lax.rem(lax.div(mi, m), 2) for m in hops]
-    starts, arrive = [0], [0]
-    for n in range(levels):
-        starts.append(starts[n] + bits[n] * (jx >> (n + 1)))
-        arrive.append(arrive[n] + (jx >> (n + 1)))
-
-    def across_ia(n):
-        return {"ia": mi + hops[n] * (1 - 2 * bits[n])}
-
-    def z_start(b, n):
-        size = jx >> (n + 1)
-        give = pl.ds(pl.multiple_of(starts[n] + (1 - bits[n]) * size, 8), size)
-        z_cp[b, n] = remote(
-            xsum.at[b, give, :], zrecv.at[b, pl.ds(arrive[n], size), :], z_send.at[b, n],
-            z_recv.at[b, n], across_ia(n),
-        )
-
-    def z_finish(b, n):
-        size = jx >> (n + 1)
-        z_cp[b, n].wait_recv()
-        keep = pl.ds(pl.multiple_of(starts[n + 1], 8), size)
-        return keep, xsum[b, keep, :] + zrecv[b, pl.ds(arrive[n], size), :]
-
-    def p_start(b, n):
-        rs = pl.ds(pl.multiple_of(b * jb + mk * jx + starts[n + 1], 8), jx >> (n + 1))
-        p_cp[b, n] = remote(
-            mfull.at[rs, :], mfull.at[rs, :], p_send.at[b, n], p_recv.at[b, n], across_ia(n)
-        )
+            sends.append(q_cp[b, d])
 
     def second(b):
-        total = mloc[pl.ds(pl.multiple_of(b * jb + mk * jx, 8), jx), :]
+        total = mloc[own_rows(b, 0, jx), :]
         for d in range(1, nk):
             x_cp[b, d].wait_recv()
             total = total + xrecv[b, d - 1]
         xsum[b] = total
-        z_start(b, 0)
-
-    def reduce_more(b):
-        for n in range(levels - 1):
-            keep, value = z_finish(b, n)
-            xsum[b, keep, :] = value
-            z_start(b, n + 1)
+
+        @pl.when(jnp.logical_not(has_outer))
+        def _():
+            fold_cp[b].start()
+
+    def fold(b):
+        @pl.when(has_outer)
+        def _():
+            fold_cp[b].wait_recv()
+            xsum[b] = xsum[b] + zrecv[b]
+
+            @pl.when(is_center)
+            def _():
+                part_cp[b].start()
+
+            @pl.when(jnp.logical_not(is_center))
+            def _():
+                fold_cp[b].start()
 
     def third(b):
-        _, total = z_finish(b, levels - 1)
-        rs = pl.ds(pl.multiple_of(b * jb + mk * jx + starts[levels], 8), jz)
-        mfull[rs, :] = total
-        p_start(b, levels - 1)
-
-    def gather_more(b):
-        for n in range(levels - 1, 0, -1):
-            p_cp[b, n].wait_recv()
-            p_start(b, n - 1)
-
-    def fourth(b):
-        p_cp[b, 0].wait_recv()
-        rs = pl.ds(pl.multiple_of(b * jb + mk * jx, 8), jx)
-        for d in range(1, nk):
-            q_cp[b, d] = remote(
-                mfull.at[rs, :], mfull.at[rs, :], q_send.at[b, d - 1], q_recv.at[b, d - 1],
-                peer("ka", mk, nk, d),
-            )
-
-    out_cp = []
-
-    def fifth(b):
-        for d in range(1, nk):
-            q_cp[b, d].wait_recv()
-        rs = pl.ds(b * jb, jb)
+        @pl.when(is_center)
+        def _():
+            part_cp[b].wait_recv()
+            mine = xsum[b, pl.ds(pl.multiple_of(keep, 8), jh), :] + zhalf[b]
+            mfull[own_rows(b, keep, jh), :] = mine
+            half_cp[b].start()
+
+    def center_done(b):
+        @pl.when(is_center)
+        def _():
+            half_cp[b].wait_recv()
+            unfold_cp[b].start()
+            for d in range(1, nk):
+                q_cp[b, d].start()
+
+    def outer_done(b):
+        @pl.when(jnp.logical_not(is_center))
+        def _():
+            unfold_cp[b].wait_recv()
+
+            @pl.when(has_outer)
+            def _():
+                unfold_cp[b].start()
+
+            for d in range(1, nk):
+                q_cp[b, d].start()
+
+    def settle(b):
+        @pl.when(jnp.logical_not(is_center))
+        def _():
+            fold_cp[b].wait_send()
+
+        @pl.when(is_center)
+        def _():
+            part_cp[b].wait_send()
+            half_cp[b].wait_send()
+
+        @pl.when(has_outer)
+        def _():
+            unfold_cp[b].wait_send()
+
+    def fifth(g):
+        for b in range(g * per, g * per + per):
+            for d in range(1, nk):
+                q_cp[b, d].wait_recv()
+        rs = pl.ds(g * jg, jg)
         value = mm_packed(mfull[rs, :], inv_a[...], inv_b[...])
-        bfull[rs, :] = value
+        b_out[rs, :] = value
         gram = mtm(value)
-        g1[...] = gram if b == 0 else g1[...] + gram
+        g1[...] = gram if g == 0 else g1[...] + gram
         return value
 
-    def sixth(b, value):
-        rs = pl.ds(b * jb, jb)
+    def sixth(g, value):
+        rs = pl.ds(g * jg, jg)
         for k in range(kl):
             s = jnp.sum(part[k, rs, :] * value, axis=0, keepdims=True)
             acc_ref[pl.ds(k, 1), :] = acc_ref[pl.ds(k, 1), :] + s
-        cp = pltpu.make_async_copy(bfull.at[rs, :], b_out.at[rs, :], o_sem.at[b])
-        cp.start()
-        out_cp.append(cp)
-
-    ahead = min(2, blocks)
+
+    ahead = min(2, groups)
     for b in range(ahead):
         first(b)
     pl.semaphore_wait(barrier, ni + nj + nk - 3)
@@ -422,7 +465,14 @@
         for _ in range(count):
             next(side)
 
-    for name, b in plan(blocks, units):
+    stages = {
+        "second": second,
+        "fold": fold,
+        "third": third,
+        "center_done": center_done,
+        "outer_done": outer_done,
+    }
+    for name, b in plan(blocks, groups, units):
         if name == "first":
             if b >= ahead:
                 first(b)
@@ -437,36 +487,35 @@
             advance(left)
             left = 0
             value = fifth(b)
-            if b + 1 < blocks:
+            if b + 1 < groups:
                 sixth(b, value)
         else:
-            {
-                "second": second,
-                "reduce_more": reduce_more,
-                "third": third,
-                "gather_more": gather_more,
-                "fourth": fourth,
-            }[name](b)
-
+            stages[name](b)
+
+    early = list(sends)
+    sends.clear()
     half = rank // 2
     low = lax.rem(mj, 2)
     mine = pl.ds(pl.multiple_of(low * half, 8), half)
     other = pl.ds(pl.multiple_of((1 - low) * half, 8), half)
     partner = {"ja": mj + 1 - 2 * low}
     cp = remote(g1.at[other, :], g_in.at[0], g_send.at[0], g_recv.at[0], partner)
-    sixth(blocks - 1, value)
-    mc_all[mi * nj + mj] = acc_ref[...]
-    mc_cp = []
-    for d in range(ni):
-        for e in range(nj):
-            if d + e:
-                where = {**peer("ia", mi, ni, d), **peer("ja", mj, nj, e)}
-                n = d * nj + e - 1
-                slot = mc_all.at[mi * nj + mj]
-                mc_cp.append(remote(slot, slot, mc_send.at[n], mc_recv.at[n], where))
+    sixth(groups - 1, value)
     cp.wait_recv()
     total = g1[mine, :] + g_in[0]
     level = 1
+    mc_cp = []
+
+    def send_c():
+        mc_all[mi * nj + mj] = acc_ref[...]
+        for d in range(ni):
+            for e in range(nj):
+                if d + e:
+                    where = {**peer("ia", mi, ni, d), **peer("ja", mj, nj, e)}
+                    n = d * nj + e - 1
+                    slot = mc_all.at[mi * nj + mj]
+                    mc_cp.append(remote(slot, slot, mc_send.at[n], mc_recv.at[n], where))
+
     while 2**level < nj:
         hop = 2**level
         bit = lax.rem(lax.div(mj, hop), 2)
@@ -475,11 +524,26 @@
             g_out.at[level - 1], g_in.at[level], g_send.at[level], g_recv.at[level],
             {"ja": mj + hop * (1 - 2 * bit)},
         )
+        if level == 1:
+            send_c()
+            for b in range(blocks):
+                settle(b)
+            for one in early:
+                one.wait_send()
         cp.wait_recv()
         total = total + g_in[level]
         level += 1
+    if level == 1:
+        send_c()
+        for b in range(blocks):
+            settle(b)
+        for one in early:
+            one.wait_send()
     g3[mine, :] = total
     cp = remote(g3.at[mine, :], g3.at[mine, :], g_send.at[level], g_recv.at[level], partner)
+    for one in sends[:-1]:
+        one.wait_send()
+    sends[:] = sends[-1:]
     cp.wait_recv()
     h = ga_full[...] * g3[...]
     down, across = scales(h)
@@ -491,44 +555,29 @@
     for n in range(1, ni * nj):
         mttkrp_c = mttkrp_c + mc_all[n]
     c_out[...] = mm_packed(mttkrp_c, first_w, second_w)[:kl, :]
-    for cp in out_cp:
-        cp.wait()
     for cp in sends:
         cp.wait_send()
 
 
-def pass_on(pieces, b_in, c_in, b_out, c_out, b_ref, c_ref, load, store):
-    size = b_ref.shape[0] // pieces
-    cuts = [pl.ds(n * size, size) for n in range(pieces)]
-    moves = [(b_in.at[cut, :], b_ref.at[cut, :], b_out.at[cut, :]) for cut in cuts]
-    moves.insert(0, (c_in, c_ref, c_out))
-    loads = [pltpu.make_async_copy(m[0], m[1], load.at[n]) for n, m in enumerate(moves)]
-    stores = [pltpu.make_async_copy(m[1], m[2], store.at[n]) for n, m in enumerate(moves)]
-    for cp in loads:
+def pass_on(b_ref, c_ref, b_out, c_out, sems):
+    pairs = ((c_ref, c_out), (b_ref, b_out))
+    moves = [pltpu.make_async_copy(src, dst, sems.at[n]) for n, (src, dst) in enumerate(pairs)]
+    for cp in moves:
         cp.start()
-    for one, two in zip(loads, stores):
-        one.wait()
-        two.start()
-    for cp in stores:
+    for cp in moves:
         cp.wait()
 
 
 def deliver(b, c):
-    pieces = 4
     hbm = pl.BlockSpec(memory_space=pltpu.HBM)
-    dma = pltpu.SemaphoreType.DMA
+    vmem = pl.BlockSpec(memory_space=pltpu.VMEM)
     return pl.pallas_call(
-        functools.partial(pass_on, pieces),
+        pass_on,
         out_shape=(jax.ShapeDtypeStruct(b.shape, b.dtype), jax.ShapeDtypeStruct(c.shape, c.dtype)),
-        in_specs=[hbm, hbm],
+        in_specs=[vmem, vmem],
         out_specs=(hbm, hbm),
-        scratch_shapes=[
-            pltpu.VMEM(b.shape, b.dtype),
-            pltpu.VMEM(c.shape, c.dtype),
-            dma((pieces + 1,)),
-            dma((pieces + 1,)),
-        ],
-        compiler_params=pltpu.CompilerParams(vmem_limit_bytes=60 * 1024 * 1024),
+        scratch_shapes=[pltpu.SemaphoreType.DMA((2,))],
+        compiler_params=pltpu.CompilerParams(vmem_limit_bytes=4 * 1024 * 1024),
     )(b, c)
 
 
@@ -536,25 +585,23 @@
     ni, nj, nk = dims
     rows, kl, il = tensor.shape
     rank = factor_a.shape[1]
-    blocks = min(8, rows // (8 * nk * ni))
+    blocks = min(NB, rows // (16 * nk))
+    groups = min(8, blocks)
     levels = (nj - 1).bit_length()
     jb = rows // blocks
     jx = jb // nk
-    jz = jx // ni
+    jg = rows // groups
+    per = blocks // groups
     kp = -(-kl // 8) * 8
-    hops = (ni - 1).bit_length()
     strip = rank // nj
     f32 = jnp.float32
     dma = pltpu.SemaphoreType.DMA
     vmem = pl.BlockSpec(memory_space=pltpu.VMEM)
     b, c = pl.pallas_call(
-        functools.partial(kernel, dims, blocks),
-        out_shape=(
-            jax.ShapeDtypeStruct((rows, rank), f32),
-            jax.ShapeDtypeStruct((kl, rank), f32),
-        ),
+        functools.partial(kernel, dims, blocks, groups),
+        out_shape=(pltpu.VMEM((rows, rank), f32), pltpu.VMEM((kl, rank), f32)),
         in_specs=[pl.BlockSpec(memory_space=pltpu.HBM)] * 4,
-        out_specs=(pl.BlockSpec(memory_space=pl.ANY), vmem),
+        out_specs=(vmem, vmem),
         scratch_shapes=[
             pltpu.VMEM((kl, rows, il), f32),
             pltpu.VMEM((kl, rows, rank), f32),
@@ -562,7 +609,7 @@
             pltpu.VMEM((blocks, nk - 1, jx, rank), f32),
             pltpu.VMEM((blocks, jx, rank), f32),
             pltpu.VMEM((blocks, jx, rank), f32),
-            pltpu.VMEM((rows, rank), f32),
+            pltpu.VMEM((blocks, jx // 2, rank), f32),
             pltpu.VMEM((rows, rank), f32),
             pltpu.VMEM((rank, rank), f32),
             pltpu.VMEM((ni, strip, rank), f32),
@@ -578,13 +625,13 @@
             pltpu.VMEM((il, rank), f32),
             pltpu.VMEM((kl, rank), f32),
             pltpu.VMEM((rank, rank), f32),
-            dma((blocks, kl)),
+            dma((groups, kl)),
             dma((blocks, nk - 1)),
             dma((blocks, nk - 1)),
-            dma((blocks, hops)),
-            dma((blocks, hops)),
-            dma((blocks, hops)),
-            dma((blocks, hops)),
+            dma((blocks, 2)),
+            dma((blocks, 2)),
+            dma((blocks, 2)),
+            dma((blocks, 2)),
             dma((blocks, nk - 1)),
             dma((blocks, nk - 1)),
             dma((ni - 1,)),
@@ -595,11 +642,10 @@
             dma((levels + 1,)),
             dma((ni * nj - 1,)),
             dma((ni * nj - 1,)),
-            dma((blocks,)),
             dma((3,)),
         ],
         compiler_params=pltpu.CompilerParams(
-            collective_id=0, has_side_effects=True, vmem_limit_bytes=60 * 1024 * 1024
+            collective_id=0, has_side_effects=True, vmem_limit_bytes=KL
         ),
     )(tensor, factor_a, factor_c, gram_c)
     return deliver(b, c)

time: 54.2 us -> 48.2 us (0.89)
  Pallas kernels: 53.4 us -> 47.2 us
    pallas_call x2, Pallas kernels: 53.4 us -> 47.2 us  [the longest x1 46.2 us: body(): pl.pallas_call(functools.partial(kernel, dims, blocks, groups), out_shape...]
where the time goes in v2:
time: 48.2 us; the launch traced here: 48 us
  Pallas kernels  47.2 us (98%)
  between operations  0.8 us (2%)
    pallas_call x1, Pallas kernels, body(): pl.pallas_call(functools.partial(kernel, dims, blocks, groups), out_shape...  46.2 us
    pallas_call x1, Pallas kernels, deliver(): pl.pallas_call(pass_on, out_shape=(jax.ShapeDtypeStruct(b.shape, b.dtype)...  0.99 us

profile of v2, /device:TPU:0, one launch (start us, length us, event | category | flops | bytes accessed | tf_op | source)
XLA Modules:
  0.0 48.0 jit_solution(11498455246932334174)
XLA Ops:
  0.6 46.2 %shard_map.59 = (f32[2048,128]{1,0:T(8,128)S(1)}, f32[4,128]{1,0:T(4,128)S(1)}) custom-call(f32[2048,4,256]{2,1,0:T(4,128)} %t_hbm.1, f32[256,128]{1,0:T(8,128)} %a_hbm.1, f32[4,128]{1,0:T(4,128)} %c_hbm.1, f32[128,128]{1,0:T(8,128)} %gc_hbm.1), custom_call_target="tpu_custom_call" | custom-call | tf_op jit(solution)/shard_map/pallas_call | solution.py:600
  46.9 1.0 %shard_map.60 = (f32[2048,128]{1,0:T(8,128)}, f32[4,128]{1,0:T(4,128)}) custom-call(f32[2048,128]{1,0:T(8,128)S(1)} %get-tuple-element.4.b_ref, f32[4,128]{1,0:T(4,128)S(1)} %get-tuple-element.5.c_ref), custom_call_target="tpu_custom_call" | custom-call | tf_op jit(solution)/shard_map/pallas_call | solution.py:574

commit v3 on v2

--- a/solution.py
+++ b/solution.py
@@ -12,7 +12,7 @@
 PANEL = 64
 WARM, FIRST, BEGIN, X_TIME, HOP = 2.0, 3.7, 3.0, 11.4, 2.5
 LAG = (3.2, 3.2, 3.2, 3.2, 0.0)
-REDUCE_AT, GRAM_AT, UNIT = 6.3, 9.5, 0.35
+REDUCE_AT, GRAM_AT, UNIT = 8, 12, 0.35
 PIECE = 8
 NB = 16
 KL = 56 * 1024 * 1024
@@ -190,7 +190,6 @@
     z_send,
     z_recv,
     p_send,
-    p_recv,
     q_send,
     q_recv,
     ga_send,
@@ -210,7 +209,6 @@
     jg = rows // groups
     per = blocks // groups
     mi, mj, mk = lax.axis_index("ia"), lax.axis_index("ja"), lax.axis_index("ka")
-    sends = []
 
     def peer(axis, me, n, d):
         return {axis: lax.rem(me + d, n)}
@@ -223,21 +221,24 @@
     def remote(src, dst, ss, rs, who):
         cp = planned(src, dst, ss, rs, who)
         cp.start()
-        sends.append(cp)
         return cp
+
+    def drained(ref, sem):
+        planned(ref, ref, sem, sem, {"ka": mk}).wait_send()
+
+    def landed(ref, sem):
+        planned(ref, ref, sem, sem, {"ka": mk}).wait_recv()
 
     icopies = []
     for n, (src, dst) in enumerate(((a_hbm, a_ref), (c_hbm, c_ref), (gc_hbm, gc_ref))):
         cp = pltpu.make_async_copy(src, dst, i_sem.at[n])
         cp.start()
         icopies.append(cp)
-    tcopies = {}
     for b in range(groups):
         for k in range(kl):
             rs = pl.ds(b * jg, jg)
-            cp = pltpu.make_async_copy(t_hbm.at[rs, k, :], tbuf.at[k, rs, :], t_sem.at[b, k])
+            cp = pltpu.make_async_copy(t_hbm.at[rs, k, :], tbuf.at[k, rs, :], t_sem.at[b])
             cp.start()
-            tcopies[b, k] = cp
 
     barrier = pltpu.get_barrier_semaphore()
     for d in range(1, ni):
@@ -259,8 +260,8 @@
     step = min(256, jg)
 
     def first(b):
-        for k in range(kl):
-            tcopies[b, k].wait()
+        piece = tbuf.at[:, pl.ds(b * jg, jg), :]
+        pltpu.make_async_copy(piece, piece, t_sem.at[b]).wait()
 
         def chunk(s, carry):
             rs = pl.ds(pl.multiple_of(b * jg + s * step, step), step)
@@ -287,7 +288,7 @@
                 other = lax.rem(mk + d, nk)
                 rs = pl.ds(pl.multiple_of(b * jb + other * jx, 8), jx)
                 x_cp[b, d] = remote(
-                    mloc.at[rs, :], xrecv.at[b, d - 1], x_send.at[b, d - 1], x_recv.at[b, d - 1],
+                    mloc.at[rs, :], xrecv.at[b, d - 1], x_send, x_recv.at[b, d - 1],
                     peer("ka", mk, nk, d),
                 )
 
@@ -307,26 +308,25 @@
     fold_cp, part_cp, half_cp, unfold_cp = {}, {}, {}, {}
     for b in range(blocks):
         fold_cp[b] = planned(
-            xsum.at[b], zrecv.at[b], z_send.at[b, 0], z_recv.at[b, 0], inward
+            xsum.at[b], zrecv.at[b], z_send.at[0], z_recv.at[b, 0], inward
         )
         part_cp[b] = planned(
             xsum.at[b, pl.ds(pl.multiple_of(give, 8), jh), :], zhalf.at[b],
-            z_send.at[b, 1], z_recv.at[b, 1], across,
+            z_send.at[1], z_recv.at[b, 1], across,
         )
         rs = own_rows(b, keep, jh)
         half_cp[b] = planned(
-            mfull.at[rs, :], mfull.at[rs, :], p_send.at[b, 0], p_recv.at[b, 0], across
+            mfull.at[rs, :], mfull.at[rs, :], p_send.at[0], z_recv.at[b, 0], across
         )
         rs = own_rows(b, 0, jx)
         unfold_cp[b] = planned(
-            mfull.at[rs, :], mfull.at[rs, :], p_send.at[b, 1], p_recv.at[b, 1], outward
+            mfull.at[rs, :], mfull.at[rs, :], p_send.at[1], x_recv.at[b, 0], outward
         )
         for d in range(1, nk):
             q_cp[b, d] = planned(
-                mfull.at[rs, :], mfull.at[rs, :], q_send.at[b, d - 1], q_recv.at[b, d - 1],
+                mfull.at[rs, :], mfull.at[rs, :], q_send, q_recv.at[b // per, d - 1],
                 peer("ka", mk, nk, d),
             )
-            sends.append(q_cp[b, d])
 
     def second(b):
         total = mloc[own_rows(b, 0, jx), :]
@@ -381,24 +381,28 @@
             for d in range(1, nk):
                 q_cp[b, d].start()
 
-    def settle(b):
+    def settle():
+        drained(xrecv, x_send)
+        drained(xrecv, q_send)
+        drained(ga_in.at[pl.ds(0, ni - 1)], ga_send)
+        drained(ga_full.at[pl.ds(0, (nj - 1) * strip), :], gf_send)
+
         @pl.when(jnp.logical_not(is_center))
         def _():
-            fold_cp[b].wait_send()
+            drained(zrecv, z_send.at[0])
 
         @pl.when(is_center)
         def _():
-            part_cp[b].wait_send()
-            half_cp[b].wait_send()
+            drained(zhalf, z_send.at[1])
+            drained(zhalf, p_send.at[0])
 
         @pl.when(has_outer)
         def _():
-            unfold_cp[b].wait_send()
+            drained(zrecv, p_send.at[1])
 
     def fifth(g):
-        for b in range(g * per, g * per + per):
-            for d in range(1, nk):
-                q_cp[b, d].wait_recv()
+        for d in range(1, nk):
+            landed(mfull.at[pl.ds(0, per * jx), :], q_recv.at[g, d - 1])
         rs = pl.ds(g * jg, jg)
         value = mm_packed(mfull[rs, :], inv_a[...], inv_b[...])
         b_out[rs, :] = value
@@ -419,36 +423,26 @@
     strip = rank // nj
     part_rows = pl.ds(pl.multiple_of(mj * strip, 8), strip)
     ga_in[mi] = ga_loc[part_rows, :]
-    ga_cp = [
+    for d in range(1, ni):
         remote(
-            ga_loc.at[part_rows, :], ga_in.at[mi], ga_send.at[d - 1], ga_recv.at[d - 1],
-            peer("ia", mi, ni, d),
+            ga_loc.at[part_rows, :], ga_in.at[mi], ga_send, ga_recv, peer("ia", mi, ni, d)
         )
-        for d in range(1, ni)
-    ]
     for b in range(ahead):
         send_first(b)
-    gf_cp = []
     state = {}
 
     def gram_reduce():
-        for cp in ga_cp:
-            cp.wait_recv()
+        landed(ga_in.at[pl.ds(0, ni - 1)], ga_recv)
         total = ga_in[0]
         for d in range(1, ni):
             total = total + ga_in[d]
         ga_full[part_rows, :] = total
         for d in range(1, nj):
-            gf_cp.append(
-                remote(
-                    ga_full.at[part_rows, :], ga_full.at[part_rows, :], gf_send.at[d - 1],
-                    gf_recv.at[d - 1], peer("ja", mj, nj, d),
-                )
-            )
+            rows_here = ga_full.at[part_rows, :]
+            remote(rows_here, rows_here, gf_send, gf_recv, peer("ja", mj, nj, d))
 
     def side_steps():
-        for cp in gf_cp:
-            cp.wait_recv()
+        landed(ga_full.at[pl.ds(0, (nj - 1) * strip), :], gf_recv)
         h = ga_full[...] * gc_ref[...]
         down, across = scales(h)
         for h in inverse_steps(h * down * across):
@@ -492,19 +486,17 @@
         else:
             stages[name](b)
 
-    early = list(sends)
-    sends.clear()
     half = rank // 2
     low = lax.rem(mj, 2)
     mine = pl.ds(pl.multiple_of(low * half, 8), half)
     other = pl.ds(pl.multiple_of((1 - low) * half, 8), half)
     partner = {"ja": mj + 1 - 2 * low}
     cp = remote(g1.at[other, :], g_in.at[0], g_send.at[0], g_recv.at[0], partner)
+    hops = [cp]
     sixth(groups - 1, value)
     cp.wait_recv()
     total = g1[mine, :] + g_in[0]
     level = 1
-    mc_cp = []
 
     def send_c():
         mc_all[mi * nj + mj] = acc_ref[...]
@@ -512,9 +504,8 @@
             for e in range(nj):
                 if d + e:
                     where = {**peer("ia", mi, ni, d), **peer("ja", mj, nj, e)}
-                    n = d * nj + e - 1
                     slot = mc_all.at[mi * nj + mj]
-                    mc_cp.append(remote(slot, slot, mc_send.at[n], mc_recv.at[n], where))
+                    remote(slot, slot, mc_send, mc_recv, where)
 
     while 2**level < nj:
         hop = 2**level
@@ -524,39 +515,33 @@
             g_out.at[level - 1], g_in.at[level], g_send.at[level], g_recv.at[level],
             {"ja": mj + hop * (1 - 2 * bit)},
         )
+        hops.append(cp)
         if level == 1:
             send_c()
-            for b in range(blocks):
-                settle(b)
-            for one in early:
-                one.wait_send()
+            settle()
         cp.wait_recv()
         total = total + g_in[level]
         level += 1
     if level == 1:
         send_c()
-        for b in range(blocks):
-            settle(b)
-        for one in early:
-            one.wait_send()
+        settle()
     g3[mine, :] = total
     cp = remote(g3.at[mine, :], g3.at[mine, :], g_send.at[level], g_recv.at[level], partner)
-    for one in sends[:-1]:
+    others = mc_all.at[pl.ds(0, ni * nj - 1)]
+    drained(others, mc_send)
+    for one in hops:
         one.wait_send()
-    sends[:] = sends[-1:]
     cp.wait_recv()
     h = ga_full[...] * g3[...]
     down, across = scales(h)
     h = h * down * across
     first_w, second_w = pack_right(inverse(h) * down * across)
-    for cp in mc_cp:
-        cp.wait_recv()
+    landed(others, mc_recv)
     mttkrp_c = mc_all[0]
     for n in range(1, ni * nj):
         mttkrp_c = mttkrp_c + mc_all[n]
     c_out[...] = mm_packed(mttkrp_c, first_w, second_w)[:kl, :]
-    for cp in sends:
-        cp.wait_send()
+    cp.wait_send()
 
 
 def pass_on(b_ref, c_ref, b_out, c_out, sems):
@@ -625,23 +610,22 @@
             pltpu.VMEM((il, rank), f32),
             pltpu.VMEM((kl, rank), f32),
             pltpu.VMEM((rank, rank), f32),
-            dma((groups, kl)),
+            dma((groups,)),
+            dma,
             dma((blocks, nk - 1)),
-            dma((blocks, nk - 1)),
+            dma((2,)),
             dma((blocks, 2)),
-            dma((blocks, 2)),
-            dma((blocks, 2)),
-            dma((blocks, 2)),
-            dma((blocks, nk - 1)),
-            dma((blocks, nk - 1)),
-            dma((ni - 1,)),
-            dma((ni - 1,)),
-            dma((nj - 1,)),
-            dma((nj - 1,)),
+            dma((2,)),
+            dma,
+            dma((groups, nk - 1)),
+            dma,
+            dma,
+            dma,
+            dma,
             dma((levels + 1,)),
             dma((levels + 1,)),
-            dma((ni * nj - 1,)),
-            dma((ni * nj - 1,)),
+            dma,
+            dma,
             dma((3,)),
         ],
         compiler_params=pltpu.CompilerParams(

time: 48.2 us -> 46.1 us (0.956)
  Pallas kernels: 47.2 us -> 45.1 us
    pallas_call x1, Pallas kernels: 46.2 us -> 44.1 us  [body(): pl.pallas_call(functools.partial(kernel, dims, blocks, groups), out_shape...]
where the time goes in v3:
time: 46.1 us; the launch traced here: 45.9 us
  Pallas kernels  45.1 us (98%)
  between operations  0.8 us (2%)
    pallas_call x1, Pallas kernels, body(): pl.pallas_call(functools.partial(kernel, dims, blocks, groups), out_shape...  44.1 us
    pallas_call x1, Pallas kernels, deliver(): pl.pallas_call(pass_on, out_shape=(jax.ShapeDtypeStruct(b.shape, b.dtype)...  0.99 us

profile of v3, /device:TPU:0, one launch (start us, length us, event | category | flops | bytes accessed | tf_op | source)
XLA Modules:
  0.0 45.9 jit_solution(11985031411412425665)
XLA Ops:
  0.6 44.1 %shard_map.59 = (f32[2048,128]{1,0:T(8,128)S(1)}, f32[4,128]{1,0:T(4,128)S(1)}) custom-call(f32[2048,4,256]{2,1,0:T(4,128)} %t_hbm.1, f32[256,128]{1,0:T(8,128)} %a_hbm.1, f32[4,128]{1,0:T(4,128)} %c_hbm.1, f32[128,128]{1,0:T(8,128)} %gc_hbm.1), custom_call_target="tpu_custom_call" | custom-call | tf_op jit(solution)/shard_map/pallas_call | solution.py:585
  44.8 1.0 %shard_map.60 = (f32[2048,128]{1,0:T(8,128)}, f32[4,128]{1,0:T(4,128)}) custom-call(f32[2048,128]{1,0:T(8,128)S(1)} %get-tuple-element.4.b_ref, f32[4,128]{1,0:T(4,128)S(1)} %get-tuple-element.5.c_ref), custom_call_target="tpu_custom_call" | custom-call | tf_op jit(solution)/shard_map/pallas_call | solution.py:559

commit v4 on v3

--- a/solution.py
+++ b/solution.py
@@ -15,6 +15,7 @@
 REDUCE_AT, GRAM_AT, UNIT = 8, 12, 0.35
 PIECE = 8
 NB = 16
+LEG = 4.0
 KL = 56 * 1024 * 1024
 
 
@@ -119,7 +120,8 @@
     return a
 
 
-def plan(blocks, groups, units):
+def plan(blocks, groups, units, legs):
+    quarter = max(1, blocks // 4)
     pace = X_TIME / blocks
     events = []
     ready = [0.0] * blocks
@@ -131,12 +133,17 @@
         for n, name in enumerate(("second", "fold", "third", "center_done", "outer_done")):
             events.append((t, b, name, b))
             ready[b] = t
+            if name == "third" and b % quarter == quarter - 1:
+                events.append((max(t, GRAM_AT + units * UNIT) + 0.1, blocks, "own_gram", b // quarter))
+                last = events[-1][0]
             t += LAG[n]
     link = BEGIN + X_TIME
     for b in range(blocks):
         link = max(link, ready[b]) + pace
         if b % per == per - 1:
             events.append((link + HOP, b, "fifth", b // per))
+    for n in range(legs):
+        events.append((last + 0.1 + LEG * n, blocks, "leg", n))
     events.append((REDUCE_AT, blocks, "gram_reduce", None))
     for n in range(units):
         events.append((GRAM_AT + n * UNIT, blocks, "side", None))
@@ -175,7 +182,6 @@
     ga_full,
     g1,
     g_in,
-    g_out,
     g3,
     mc_all,
     inv_a,
@@ -406,8 +412,6 @@
         rs = pl.ds(g * jg, jg)
         value = mm_packed(mfull[rs, :], inv_a[...], inv_b[...])
         b_out[rs, :] = value
-        gram = mtm(value)
-        g1[...] = gram if g == 0 else g1[...] + gram
         return value
 
     def sixth(g, value):
@@ -415,6 +419,62 @@
         for k in range(kl):
             s = jnp.sum(part[k, rs, :] * value, axis=0, keepdims=True)
             acc_ref[pl.ds(k, 1), :] = acc_ref[pl.ds(k, 1), :] + s
+
+    quarter = max(1, blocks // 4)
+    owners = 2 * nj * nk
+    share = rank // owners
+
+    def owner_at(ia, ja, ka):
+        return (jnp.where(ia < middle, 0, nj) + ja) * nk + ka
+
+    def share_of(n):
+        return pl.ds(pl.multiple_of(n * share, 8), share)
+
+    me = owner_at(mi, mj, mk)
+    gather_cp, spread_cp = [], []
+    for ia in (mi, ni - 1 - mi):
+        for e in range(nj):
+            for f in range(nk):
+                if ia is mi and e + f == 0:
+                    continue
+                where = {"ia": ia, **peer("ja", mj, nj, e), **peer("ka", mk, nk, f)}
+                to = owner_at(ia, where["ja"], where["ka"])
+                gather_cp.append(
+                    planned(g1.at[share_of(to), :], g_in.at[me], g_send.at[0], g_recv.at[0], where)
+                )
+    for d in range(ni):
+        for e in range(nj):
+            for f in range(nk):
+                if d + e + f:
+                    where = {
+                        **peer("ia", mi, ni, d), **peer("ja", mj, nj, e), **peer("ka", mk, nk, f)
+                    }
+                    piece = g3.at[share_of(me), :]
+                    spread_cp.append(planned(piece, piece, g_send.at[1], g_recv.at[1], where))
+
+    def own_gram(q):
+        @pl.when(is_center)
+        def _():
+            some = range(q * quarter, q * quarter + quarter)
+            known = jnp.concatenate([mfull[own_rows(b, keep, jh), :] for b in some], axis=0)
+            gram = mtm(mm_packed(known, inv_a[...], inv_b[...]))
+            g1[...] = gram if q == 0 else g1[...] + gram
+
+    def leg(n):
+        @pl.when(is_center)
+        def _():
+            if n == 0:
+                for cp in gather_cp:
+                    cp.start()
+                g_in[me] = g1[share_of(me), :]
+            else:
+                landed(g_in.at[pl.ds(0, owners - 1)], g_recv.at[0])
+                total = g_in[0]
+                for m in range(1, owners):
+                    total = total + g_in[m]
+                g3[share_of(me), :] = total
+                for cp in spread_cp:
+                    cp.start()
 
     ahead = min(2, groups)
     for b in range(ahead):
@@ -465,8 +525,9 @@
         "third": third,
         "center_done": center_done,
         "outer_done": outer_done,
+        "leg": leg,
     }
-    for name, b in plan(blocks, groups, units):
+    for name, b in plan(blocks, groups, units, 2):
         if name == "first":
             if b >= ahead:
                 first(b)
@@ -477,71 +538,54 @@
             if left:
                 advance(1)
                 left -= 1
-        elif name == "fifth":
+        elif name in ("fifth", "own_gram"):
             advance(left)
             left = 0
+            if name == "own_gram":
+                own_gram(b)
+                continue
             value = fifth(b)
             if b + 1 < groups:
                 sixth(b, value)
         else:
             stages[name](b)
 
-    half = rank // 2
-    low = lax.rem(mj, 2)
-    mine = pl.ds(pl.multiple_of(low * half, 8), half)
-    other = pl.ds(pl.multiple_of((1 - low) * half, 8), half)
-    partner = {"ja": mj + 1 - 2 * low}
-    cp = remote(g1.at[other, :], g_in.at[0], g_send.at[0], g_recv.at[0], partner)
-    hops = [cp]
     sixth(groups - 1, value)
-    cp.wait_recv()
-    total = g1[mine, :] + g_in[0]
-    level = 1
-
-    def send_c():
-        mc_all[mi * nj + mj] = acc_ref[...]
-        for d in range(ni):
-            for e in range(nj):
-                if d + e:
-                    where = {**peer("ia", mi, ni, d), **peer("ja", mj, nj, e)}
-                    slot = mc_all.at[mi * nj + mj]
-                    remote(slot, slot, mc_send, mc_recv, where)
-
-    while 2**level < nj:
-        hop = 2**level
-        bit = lax.rem(lax.div(mj, hop), 2)
-        g_out[level - 1] = total
-        cp = remote(
-            g_out.at[level - 1], g_in.at[level], g_send.at[level], g_recv.at[level],
-            {"ja": mj + hop * (1 - 2 * bit)},
-        )
-        hops.append(cp)
-        if level == 1:
-            send_c()
-            settle()
-        cp.wait_recv()
-        total = total + g_in[level]
-        level += 1
-    if level == 1:
-        send_c()
-        settle()
-    g3[mine, :] = total
-    cp = remote(g3.at[mine, :], g3.at[mine, :], g_send.at[level], g_recv.at[level], partner)
-    others = mc_all.at[pl.ds(0, ni * nj - 1)]
-    drained(others, mc_send)
-    for one in hops:
-        one.wait_send()
-    cp.wait_recv()
+    mc_all[mi * nj + mj] = acc_ref[...]
+    for d in range(ni):
+        for e in range(nj):
+            if d + e:
+                where = {**peer("ia", mi, ni, d), **peer("ja", mj, nj, e)}
+                slot = mc_all.at[mi * nj + mj]
+                remote(slot, slot, mc_send, mc_recv, where)
+
+    @pl.when(is_center)
+    def _():
+        landed(g3.at[pl.ds(0, rank - share), :], g_recv.at[1])
+
+    @pl.when(jnp.logical_not(is_center))
+    def _():
+        landed(g3, g_recv.at[1])
+
     h = ga_full[...] * g3[...]
     down, across = scales(h)
     h = h * down * across
     first_w, second_w = pack_right(inverse(h) * down * across)
+    others = mc_all.at[pl.ds(0, ni * nj - 1)]
+    settle()
+
+    @pl.when(is_center)
+    def _():
+        drained(g_in.at[pl.ds(0, owners - 1)], g_send.at[0])
+        for cp in spread_cp:
+            cp.wait_send()
+
+    drained(others, mc_send)
     landed(others, mc_recv)
     mttkrp_c = mc_all[0]
     for n in range(1, ni * nj):
         mttkrp_c = mttkrp_c + mc_all[n]
     c_out[...] = mm_packed(mttkrp_c, first_w, second_w)[:kl, :]
-    cp.wait_send()
 
 
 def pass_on(b_ref, c_ref, b_out, c_out, sems):
@@ -572,7 +616,7 @@
     rank = factor_a.shape[1]
     blocks = min(NB, rows // (16 * nk))
     groups = min(8, blocks)
-    levels = (nj - 1).bit_length()
+    owners = 2 * nj * nk
     jb = rows // blocks
     jx = jb // nk
     jg = rows // groups
@@ -600,8 +644,7 @@
             pltpu.VMEM((ni, strip, rank), f32),
             pltpu.VMEM((rank, rank), f32),
             pltpu.VMEM((rank, rank), f32),
-            pltpu.VMEM((levels, rank // 2, rank), f32),
-            pltpu.VMEM((levels, rank // 2, rank), f32),
+            pltpu.VMEM((owners, rank // owners, rank), f32),
             pltpu.VMEM((rank, rank), f32),
             pltpu.VMEM((ni * nj, kp, rank), f32),
             pltpu.VMEM((2 * rank, 2 * rank), jnp.bfloat16),
@@ -622,8 +665,8 @@
             dma,
             dma,
             dma,
-            dma((levels + 1,)),
-            dma((levels + 1,)),
+            dma((2,)),
+            dma((2,)),
             dma,
             dma,
             dma((3,)),

time: 46.1 us -> 42.4 us (0.920)
  Pallas kernels: 45.1 us -> 41.6 us
    pallas_call x1, Pallas kernels: 44.1 us -> 40.6 us  [body(): pl.pallas_call(functools.partial(kernel, dims, blocks, groups), out_shape...]
where the time goes in v4:
time: 42.4 us; the launch traced here: 42.3 us
  Pallas kernels  41.6 us (98%)
  between operations  0.64 us (2%)
    pallas_call x1, Pallas kernels, body(): pl.pallas_call(functools.partial(kernel, dims, blocks, groups), out_shape...  40.6 us
    pallas_call x1, Pallas kernels, deliver(): pl.pallas_call(pass_on, out_shape=(jax.ShapeDtypeStruct(b.shape, b.dtype)...  0.99 us

profile of v4, /device:TPU:0, one launch (start us, length us, event | category | flops | bytes accessed | tf_op | source)
XLA Modules:
  0.0 42.3 jit_solution(9789254343863307883)
XLA Ops:
  0.6 40.6 %shard_map.59 = (f32[2048,128]{1,0:T(8,128)S(1)}, f32[4,128]{1,0:T(4,128)S(1)}) custom-call(f32[2048,4,256]{2,1,0:T(4,128)} %t_hbm.1, f32[256,128]{1,0:T(8,128)} %a_hbm.1, f32[4,128]{1,0:T(4,128)} %c_hbm.1, f32[128,128]{1,0:T(8,128)} %gc_hbm.1), custom_call_target="tpu_custom_call" | custom-call | tf_op jit(solution)/shard_map/pallas_call | solution.py:629
  41.3 1.0 %shard_map.60 = (f32[2048,128]{1,0:T(8,128)}, f32[4,128]{1,0:T(4,128)}) custom-call(f32[2048,128]{1,0:T(8,128)S(1)} %get-tuple-element.4.b_ref, f32[4,128]{1,0:T(4,128)S(1)} %get-tuple-element.5.c_ref), custom_call_target="tpu_custom_call" | custom-call | tf_op jit(solution)/shard_map/pallas_call | solution.py:603

commit v5 on v4

--- a/solution.py
+++ b/solution.py
@@ -16,6 +16,7 @@
 PIECE = 8
 NB = 16
 LEG = 4.0
+SPARE, RAMP = 1.5, 1.0
 KL = 56 * 1024 * 1024
 
 
@@ -136,12 +137,12 @@
             if name == "third" and b % quarter == quarter - 1:
                 events.append((max(t, GRAM_AT + units * UNIT) + 0.1, blocks, "own_gram", b // quarter))
                 last = events[-1][0]
-            t += LAG[n]
+            t += LAG[n] * min(1.0, RAMP + (1.0 - RAMP) * b / blocks * 2)
     link = BEGIN + X_TIME
     for b in range(blocks):
         link = max(link, ready[b]) + pace
         if b % per == per - 1:
-            events.append((link + HOP, b, "fifth", b // per))
+            events.append((link + HOP + SPARE, b, "fifth", b // per))
     for n in range(legs):
         events.append((last + 0.1 + LEG * n, blocks, "leg", n))
     events.append((REDUCE_AT, blocks, "gram_reduce", None))
@@ -235,6 +236,14 @@
     def landed(ref, sem):
         planned(ref, ref, sem, sem, {"ka": mk}).wait_recv()
 
+    barrier = pltpu.get_barrier_semaphore()
+    for d in range(1, ni):
+        pl.semaphore_signal(barrier, inc=1, device_id=peer("ia", mi, ni, d), device_id_type=MESH)
+    for d in range(1, nj):
+        pl.semaphore_signal(barrier, inc=1, device_id=peer("ja", mj, nj, d), device_id_type=MESH)
+    for d in range(1, nk):
+        pl.semaphore_signal(barrier, inc=1, device_id=peer("ka", mk, nk, d), device_id_type=MESH)
+
     icopies = []
     for n, (src, dst) in enumerate(((a_hbm, a_ref), (c_hbm, c_ref), (gc_hbm, gc_ref))):
         cp = pltpu.make_async_copy(src, dst, i_sem.at[n])
@@ -246,21 +255,12 @@
             cp = pltpu.make_async_copy(t_hbm.at[rs, k, :], tbuf.at[k, rs, :], t_sem.at[b])
             cp.start()
 
-    barrier = pltpu.get_barrier_semaphore()
-    for d in range(1, ni):
-        pl.semaphore_signal(barrier, inc=1, device_id=peer("ia", mi, ni, d), device_id_type=MESH)
-    for d in range(1, nj):
-        pl.semaphore_signal(barrier, inc=1, device_id=peer("ja", mj, nj, d), device_id_type=MESH)
-    for d in range(1, nk):
-        pl.semaphore_signal(barrier, inc=1, device_id=peer("ka", mk, nk, d), device_id_type=MESH)
-
     for cp in icopies:
         cp.wait()
     a = a_ref[...]
     a_hi = a.astype(jnp.bfloat16)
     a_lo = (a - a_hi.astype(jnp.float32)).astype(jnp.bfloat16)
     weights = jnp.concatenate([a_hi, a_lo], axis=1)
-    ga_loc[...] = mtm(a)
 
     x_cp, z_cp, p_cp, q_cp = {}, {}, {}, {}
     step = min(256, jg)
@@ -476,10 +476,13 @@
                 for cp in spread_cp:
                     cp.start()
 
-    ahead = min(2, groups)
+    ahead = min(1, groups)
     for b in range(ahead):
         first(b)
     pl.semaphore_wait(barrier, ni + nj + nk - 3)
+    for b in range(ahead):
+        send_first(b)
+    ga_loc[...] = mtm(a)
     strip = rank // nj
     part_rows = pl.ds(pl.multiple_of(mj * strip, 8), strip)
     ga_in[mi] = ga_loc[part_rows, :]
@@ -487,8 +490,6 @@
         remote(
             ga_loc.at[part_rows, :], ga_in.at[mi], ga_send, ga_recv, peer("ia", mi, ni, d)
         )
-    for b in range(ahead):
-        send_first(b)
     state = {}
 
     def gram_reduce():

time: 42.4 us -> 42.2 us (level)
  no operation moved by 1% of the time
where the time goes in v5:
time: 42.2 us; the launch traced here: 42 us
  Pallas kernels  41.4 us (98%)
  between operations  0.64 us (2%)
    pallas_call x1, Pallas kernels, body(): pl.pallas_call(functools.partial(kernel, dims, blocks, groups), out_shape...  40.4 us
    pallas_call x1, Pallas kernels, deliver(): pl.pallas_call(pass_on, out_shape=(jax.ShapeDtypeStruct(b.shape, b.dtype)...  0.99 us

profile of v5, /device:TPU:0, one launch (start us, length us, event | category | flops | bytes accessed | tf_op | source)
XLA Modules:
  0.0 42.0 jit_solution(10766734072338170063)
XLA Ops:
  0.6 40.4 %shard_map.59 = (f32[2048,128]{1,0:T(8,128)S(1)}, f32[4,128]{1,0:T(4,128)S(1)}) custom-call(f32[2048,4,256]{2,1,0:T(4,128)} %t_hbm.1, f32[256,128]{1,0:T(8,128)} %a_hbm.1, f32[4,128]{1,0:T(4,128)} %c_hbm.1, f32[128,128]{1,0:T(8,128)} %gc_hbm.1), custom_call_target="tpu_custom_call" | custom-call | tf_op jit(solution)/shard_map/pallas_call | solution.py:630
  41.1 1.0 %shard_map.60 = (f32[2048,128]{1,0:T(8,128)}, f32[4,128]{1,0:T(4,128)}) custom-call(f32[2048,128]{1,0:T(8,128)S(1)} %get-tuple-element.4.b_ref, f32[4,128]{1,0:T(4,128)S(1)} %get-tuple-element.5.c_ref), custom_call_target="tpu_custom_call" | custom-call | tf_op jit(solution)/shard_map/pallas_call | solution.py:604
